TPU v7x, 32 devices: a whole 2x2x4 slice. The times are simulated.
32 devices in a mesh: dp: 2 (over x), row: 2 (over core), col: 8 (over z, y).
Axes of the slice: x: 2, y: 2, z: 4, core: 2. Of those that a mesh axis runs over, the one named last changes fastest.
Arguments:
- tokens: bfloat16 [12288, 1024], P(('dp', 'col'), 'row'), may hold values from -6 to 6
- segments: int32 [12, 1024], P(('dp', 'row')), may hold values from 0 to 17, as said below
- attend_gain: bfloat16 [1024], P('row'), may hold values from 0.5 to 1.5
- attend_shift: bfloat16 [1024], P('row'), may hold values from -1.75 to 1.75
- input_weight: bfloat16 [1024, 3, 1024], P('row', None, 'col'), may hold values from -0.1875 to 0.1875
- input_bias: bfloat16 [2, 1024], P(None, 'col'), may hold values from -3 to 3
- output_weight: bfloat16 [1024, 1024], P('col', 'row'), may hold values from -1.5 to 1.5
- output_bias: bfloat16 [1024], P('row'), may hold values from -1.75 to 1.75
- feed_gain: bfloat16 [1024], P('row'), may hold values from 0.5 to 1.5
- feed_shift: bfloat16 [1024], P('row'), may hold values from -1.75 to 1.75
- up_weight: bfloat16 [1024, 4096], P('row', 'col'), may hold values from -0.1875 to 0.1875
- up_bias: bfloat16 [4096], P('col'), may hold values from -1.75 to 1.75
- down_weight: bfloat16 [4096, 1024], P('col', 'row'), may hold values from -0.09375 to 0.09375
- down_bias: bfloat16 [1024], P('row'), may hold values from -1.75 to 1.75
- grad_out: bfloat16 [12288, 1024], P(('dp', 'col'), 'row'), may hold values from -6 to 6
Outputs:
- layer_out: bfloat16 [12288, 1024], P(('dp', 'col'), 'row')
- grad_tokens: float32 [12288, 1024], P(('dp', 'col'), 'row')
- grad_attend_gain: float32 [1024], P('row')
- grad_attend_shift: float32 [1024], P('row')
- grad_input_weight: float32 [1024, 3, 1024], P('row', None, 'col')
- grad_input_bias: float32 [2, 1024], P(None, 'col')
- grad_output_weight: float32 [1024, 1024], P('col', 'row')
- grad_output_bias: float32 [1024], P('row')
- grad_feed_gain: float32 [1024], P('row')
- grad_feed_shift: float32 [1024], P('row')
- grad_up_weight: float32 [1024, 4096], P('row', 'col')
- grad_up_bias: float32 [4096], P('col')
- grad_down_weight: float32 [4096, 1024], P('col', 'row')
- grad_down_bias: float32 [1024], P('row')
Inputs may be any that keep to these rules, and one draw needn't show every extreme that they name: `segments`: along each sequence the numbers never fall; documents are numbered 1, 2, 3 in order; every sequence ends in padding marked 0, and 0 appears nowhere else. The first sequence reaches the largest document number.
All inputs are finite; a program needn't handle non-finite values.
Results may differ from a plain program's by a relative error of at most 0.0092.
Values may be sent and summed in bfloat16 or wider, within the bound.
No kernel may reach another device: no remote copies, remote signals or barrier semaphores. Data moves between devices by JAX's collectives and lax.ppermute only.
A program may use at most 192 MiB of HBM per device.

v0:
```python
from functools import partial

import jax
import jax.numpy as jnp
from jax import lax
from jax.sharding import PartitionSpec as P

HD = 64


epsilon = 1e-05
masked_score = -1000000000.0


def for_sending(shard):

    def short(part):
        return part.astype(jnp.bfloat16) if part.dtype == jnp.float32 else part

    return jax.tree.map(short, shard)


def product(left_side, right_side, flipped):
    if flipped:
        return lax.dot_general(
            left_side, right_side, (((1,), (1,)), ((), ())), preferred_element_type=jnp.float32
        )
    return jnp.dot(left_side, right_side, preferred_element_type=jnp.float32)


def inner_rows(left_side, right_side):
    return lax.dot_general(
        left_side, right_side, (((0,), (0,)), ((), ())), preferred_element_type=jnp.float32
    )


def width_totals(first_sum, second_sum):
    return lax.psum((first_sum, second_sum), "row")


def norm_forward(values, gain, shift):
    features = values.shape[1] * lax.axis_size("row")
    totals, square = width_totals(
        jnp.sum(values, axis=1, keepdims=True), jnp.sum(values * values, axis=1, keepdims=True)
    )
    average = totals / features
    inverse = lax.rsqrt(square / features - average * average + epsilon)
    normed = (values - average) * inverse
    return (normed * gain + shift, normed, inverse)


def norm_backward(grad_norm, normed, inverse, gain):
    features = grad_norm.shape[1] * lax.axis_size("row")
    scaled = grad_norm * gain
    totals, against = width_totals(
        jnp.sum(scaled, axis=1, keepdims=True), jnp.sum(scaled * normed, axis=1, keepdims=True)
    )
    returned = inverse * (scaled - totals / features - normed * against / features)
    return (returned, jnp.sum(grad_norm * normed, axis=0), jnp.sum(grad_norm, axis=0))


def col_then_row(shard_in, weight, flipped):
    gathered = lax.all_gather(shard_in, "col", axis=0, tiled=True)
    return (
        gathered,
        lax.psum_scatter(
            product(gathered, weight, flipped), "row", scatter_dimension=0, tiled=True
        ),
    )


def row_then_col(shard_in, weight, flipped):
    gathered = lax.all_gather(for_sending(shard_in), "row", axis=0, tiled=True).astype(
        shard_in.dtype
    )
    row_count = gathered.shape[0] // lax.axis_size("col")
    block_rows = lax.dynamic_slice_in_dim(
        gathered, jnp.int32(0), lax.axis_size("col") * row_count, 0
    )
    return (
        gathered,
        lax.psum_scatter(
            product(block_rows, weight, flipped), "col", scatter_dimension=0, tiled=True
        ),
    )


def head_masks(labels):
    positions = jnp.arange(labels.shape[0])
    causal = positions[None, :] <= positions[:, None]
    matching = (labels[:, None] == labels[None, :]) & (labels[:, None] > 0)
    return causal & (matching | (positions[:, None] == positions[None, :]))


def scores_of(queries, key_rows, labels):
    scaling = queries.shape[-1] ** (-0.5)
    products = (
        jnp.einsum("qhd,khd->hqk", queries, key_rows, preferred_element_type=jnp.float32) * scaling
    )
    return jnp.where(head_masks(labels)[None], products, masked_score)


def attend_forward(packed):
    queries, key_rows, values, labels = packed
    scores = scores_of(queries, key_rows, labels)
    highest = jnp.max(scores, axis=2, keepdims=True)
    weights = jnp.exp(scores - highest)
    totals = jnp.sum(weights, axis=2, keepdims=True)
    chances = (weights / totals).astype(jnp.bfloat16)
    attended = jnp.einsum("hqk,khd->qhd", chances, values, preferred_element_type=jnp.float32)
    return (attended.astype(jnp.bfloat16), highest + jnp.log(totals))


def attend_backward(packed):
    queries, key_rows, values, labels, summary, grad_attended = packed
    scaling = queries.shape[-1] ** (-0.5)
    chances = jnp.exp(scores_of(queries, key_rows, labels) - summary)
    rounded = chances.astype(jnp.bfloat16)
    grad_values = jnp.einsum(
        "hqk,qhd->khd", rounded, grad_attended, preferred_element_type=jnp.float32
    )
    grad_chances = jnp.einsum(
        "qhd,khd->hqk", grad_attended, values, preferred_element_type=jnp.float32
    )
    grad_scores = chances * (grad_chances - jnp.sum(chances * grad_chances, axis=2, keepdims=True))
    grad_scores = grad_scores.astype(jnp.bfloat16)
    grad_queries = (
        jnp.einsum("hqk,khd->qhd", grad_scores, key_rows, preferred_element_type=jnp.float32)
        * scaling
    )
    grad_keys = (
        jnp.einsum("hqk,qhd->khd", grad_scores, queries, preferred_element_type=jnp.float32)
        * scaling
    )
    return (grad_queries, grad_keys, grad_values)


def per_device(
    tokens,
    segments,
    attend_gain,
    attend_shift,
    input_weight,
    input_bias,
    output_weight,
    output_bias,
    feed_gain,
    feed_shift,
    up_weight,
    up_bias,
    down_weight,
    down_bias,
    grad_out,
):
    inputs = tokens.astype(jnp.float32)
    seq_count, length = segments.shape
    head_width = input_weight.shape[2]
    heads_here = head_width // HD
    input_flat = input_weight.reshape(input_weight.shape[0], 3 * head_width)
    gain_one = attend_gain.astype(jnp.float32)
    gain_two = feed_gain.astype(jnp.float32)
    first_out, normed_one, inverse_one = norm_forward(
        inputs, gain_one, attend_shift.astype(jnp.float32)
    )
    first_low = first_out.astype(jnp.bfloat16)
    first_all, projected = col_then_row(first_low, input_flat, False)
    zero_row = jnp.zeros((1, head_width), jnp.float32)
    bias_rows = jnp.concatenate(
        [input_bias[0:1].astype(jnp.float32), zero_row, input_bias[1:2].astype(jnp.float32)], axis=1
    )
    projected = (projected + bias_rows).astype(jnp.bfloat16)
    shaped = projected.reshape(seq_count, length, 3, heads_here, HD)
    queries = shaped[:, :, 0]
    key_rows = shaped[:, :, 1]
    values = shaped[:, :, 2]
    attended, summary = lax.map(attend_forward, (queries, key_rows, values, segments))
    attended_flat = attended.reshape(seq_count * length, head_width)
    attended_all, branch_one = row_then_col(attended_flat, output_weight, False)
    middle = inputs + (branch_one + output_bias.astype(jnp.float32))
    second_out, normed_two, inverse_two = norm_forward(
        middle, gain_two, feed_shift.astype(jnp.float32)
    )
    second_low = second_out.astype(jnp.bfloat16)
    gelu_tanh = partial(jax.nn.gelu, approximate=True)
    second_all, hidden_pre = col_then_row(second_low, up_weight, False)
    hidden_pre = hidden_pre + up_bias.astype(jnp.float32)
    hidden = gelu_tanh(hidden_pre).astype(jnp.bfloat16)
    hidden_all, branch_two = row_then_col(hidden, down_weight, False)
    result = middle + (branch_two + down_bias.astype(jnp.float32))
    layer_out = result.astype(jnp.bfloat16)
    grad_top = grad_out.astype(jnp.float32)
    grad_down_bias = jnp.sum(grad_top, axis=0)
    output_all, grad_hidden = col_then_row(grad_out, down_weight, True)
    gelu_unused, gelu_pull = jax.vjp(gelu_tanh, hidden_pre)
    grad_pre = gelu_pull(grad_hidden)[0].astype(jnp.bfloat16)
    grad_up_bias = jnp.sum(grad_pre.astype(jnp.float32), axis=0)
    grad_down_weight = inner_rows(hidden_all, output_all)
    pre_all, grad_second = row_then_col(grad_pre, up_weight, True)
    grad_up_weight = inner_rows(second_all, pre_all)
    grad_norm_two, grad_feed_gain, grad_feed_shift = norm_backward(
        grad_second, normed_two, inverse_two, gain_two
    )
    grad_middle = grad_top + grad_norm_two
    grad_branch = grad_middle.astype(jnp.bfloat16)
    grad_output_bias = jnp.sum(grad_branch.astype(jnp.float32), axis=0)
    branch_all, grad_attended = col_then_row(grad_branch, output_weight, True)
    grad_output_weight = inner_rows(attended_all, branch_all)
    grad_heads = grad_attended.astype(jnp.bfloat16).reshape(seq_count, length, heads_here, HD)
    grad_queries, grad_keys, grad_values = lax.map(
        attend_backward, (queries, key_rows, values, segments, summary, grad_heads)
    )
    grad_projected = jnp.stack([grad_queries, grad_keys, grad_values], axis=2).astype(jnp.bfloat16)
    grad_projected = grad_projected.reshape(seq_count * length, 3 * head_width)
    slot_sums = jnp.sum(grad_projected.astype(jnp.float32), axis=0).reshape(3, head_width)
    grad_input_bias = jnp.stack([slot_sums[0], slot_sums[2]])
    projected_all, grad_first = row_then_col(grad_projected, input_flat, True)
    grad_input_weight = inner_rows(first_all, projected_all).reshape(input_weight.shape)
    grad_norm_one, grad_attend_gain, grad_attend_shift = norm_backward(
        grad_first, normed_one, inverse_one, gain_one
    )
    grad_tokens = grad_middle + grad_norm_one
    grad_input_weight, grad_output_weight, grad_up_weight, grad_down_weight = lax.psum(
        (grad_input_weight, grad_output_weight, grad_up_weight, grad_down_weight), "dp"
    )
    (
        grad_attend_gain,
        grad_attend_shift,
        grad_output_bias,
        grad_feed_gain,
        grad_feed_shift,
        grad_down_bias,
    ) = lax.psum(
        (
            grad_attend_gain,
            grad_attend_shift,
            grad_output_bias,
            grad_feed_gain,
            grad_feed_shift,
            grad_down_bias,
        ),
        ("dp", "col"),
    )
    grad_input_bias, grad_up_bias = lax.psum((grad_input_bias, grad_up_bias), ("dp", "row"))
    return (
        layer_out,
        grad_tokens,
        grad_attend_gain,
        grad_attend_shift,
        grad_input_weight,
        grad_input_bias,
        grad_output_weight,
        grad_output_bias,
        grad_feed_gain,
        grad_feed_shift,
        grad_up_weight,
        grad_up_bias,
        grad_down_weight,
        grad_down_bias,
    )


def solution(mesh):
    in_specs = (
        P(("dp", "col"), "row"),
        P(("dp", "row"), None),
        P("row"),
        P("row"),
        P("row", None, "col"),
        P(None, "col"),
        P("col", "row"),
        P("row"),
        P("row"),
        P("row"),
        P("row", "col"),
        P("col"),
        P("col", "row"),
        P("row"),
        P(("dp", "col"), "row"),
    )
    out_specs = (
        P(("dp", "col"), "row"),
        P(("dp", "col"), "row"),
        P("row"),
        P("row"),
        P("row", None, "col"),
        P(None, "col"),
        P("col", "row"),
        P("row"),
        P("row"),
        P("row"),
        P("row", "col"),
        P("col"),
        P("col", "row"),
        P("row"),
    )
    return jax.shard_map(
        per_device, mesh=mesh, in_specs=in_specs, out_specs=out_specs, check_vma=False
    )
```

profile of v0, /device:TPU:0, one launch (start us, length us, event | category | flops | bytes accessed | tf_op | source)
XLA Modules:
  0.0 1655.1 jit_solution(5159023049874539472)
XLA Ops:
  17.0 100.2 %all-gather.9.cloned.1.call-done = bf16[6144,512]{1,0:T(8,128)(2,1)} async-done(((bf16[768,512]{1,0:T(8,128)(2,1)}), bf16[6144,512]{1,0:T(8,128)(2,1)}) %all-gather.9.cloned.1.call-update) | async-done | bytes 6291472 | tf_op jit(solution)/shard_map/all_gather | solution.py:63
  117.2 9.9 fusion.84
  127.8 14.9 reduce-scatter.9.cloned.1.call-done
  148.0 7.4 reshape.240
  155.4 3.0 slice_bitcast_fusion
  159.4 30.3 %while.26 = (s32[]{:T(128)}, bf16[3,1024,2,64]{1,3,2,0:T(8,128)(2,1)}, f32[3,2,1024,1]{2,1,3,0:T(2,128)}, bf16[3,1024,2,64]{1,3,2,0:T(8,128)(2,1)S(1)}, s32[3,10...) while((s32[]{:T(128)}, ...), condition=%wide.region_8.9_spmd, body=%wide.region_5.8_spmd.sunk | while | flops 568458240 | bytes 30494820 | solution.py:176
  165.4 3.5 fusion.144
  175.5 3.5 fusion.144
  185.6 3.5 fusion.144
  193.4 11.2 all-gather.11.cloned.1.call-done
  204.6 7.7 fusion.85
  215.2 206.0 %reduce-scatter.11.cloned.1.call-done = f32[768,512]{1,0:T(8,128)} async-done(((f32[6144,512]{1,0:T(8,128)}), f32[768,512]{1,0:T(8,128)}) %reduce-scatter.11.cloned.1.call-update) | async-done | bytes 1572880 | tf_op jit(solution)/shard_map/reduce_scatter | solution.py:82
  427.5 93.5 %all-gather.17.cloned.1.call-done = bf16[6144,512]{1,0:T(8,128)(2,1)} async-done(((bf16[768,512]{1,0:T(8,128)(2,1)}), bf16[6144,512]{1,0:T(8,128)(2,1)}) %all-gather.17.cloned.1.call-update) | async-done | bytes 6291472 | tf_op jit(solution)/shard_map/all_gather | solution.py:63
  521.0 9.5 fusion.88
  530.6 89.9 %all-gather.13.cloned.1.call-done = bf16[6144,512]{1,0:T(8,128)(2,1)} async-done(((bf16[768,512]{1,0:T(8,128)(2,1)}), bf16[6144,512]{1,0:T(8,128)(2,1)}) %all-gather.13.cloned.1.call-update) | async-done | bytes 6291472 | tf_op jit(solution)/shard_map/all_gather | solution.py:63
  620.6 10.6 fusion.86
  631.9 9.9 reduce-scatter.17.cloned.1.call-done
  641.8 25.7 %reduce-scatter.13.cloned.1.call-done = f32[3072,512]{1,0:T(8,128)} async-done(((f32[6144,512]{1,0:T(8,128)}), f32[3072,512]{1,0:T(8,128)}) %reduce-scatter.13.cloned.1.call-update) | async-done | bytes 6291472 | tf_op jit(solution)/shard_map/reduce_scatter | solution.py:66
  667.5 10.0 convert_reduce_fusion
  678.2 18.7 %all-gather.19.cloned.1.call-done = bf16[6144,512]{1,0:T(8,128)(2,1)} async-done(((bf16[3072,512]{1,0:T(8,128)(2,1)}), bf16[6144,512]{1,0:T(8,128)(2,1)}) %all-gather.19.cloned.1.call-update) | async-done | bytes 6291472 | tf_op jit(solution)/shard_map/all_gather | solution.py:73
  696.8 9.5 fusion.89
  706.4 9.8 all-gather.15.cloned.1.call-done
  716.2 9.2 fusion.87
  726.1 202.3 %reduce-scatter.19.cloned.1.call-done = f32[768,512]{1,0:T(8,128)} async-done(((f32[6144,512]{1,0:T(8,128)}), f32[768,512]{1,0:T(8,128)}) %reduce-scatter.19.cloned.1.call-update) | async-done | bytes 1572880 | tf_op jit(solution)/shard_map/reduce_scatter | solution.py:82
  928.4 2.7 multiply_reduce_fusion.1
  933.8 204.6 %reduce-scatter.15.cloned.1.call-done = f32[768,512]{1,0:T(8,128)} async-done(((f32[6144,512]{1,0:T(8,128)}), f32[768,512]{1,0:T(8,128)}) %reduce-scatter.15.cloned.1.call-update) | async-done | bytes 1572880 | tf_op jit(solution)/shard_map/reduce_scatter | solution.py:82
  1138.4 3.5 convert_reduce_fusion.4
  1142.0 97.9 %all-gather.21.cloned.1.call-done = bf16[6144,512]{1,0:T(8,128)(2,1)} async-done(((bf16[768,512]{1,0:T(8,128)(2,1)}), bf16[6144,512]{1,0:T(8,128)(2,1)}) %all-gather.21.cloned.1.call-update) | async-done | bytes 6291472 | tf_op jit(solution)/shard_map/all_gather | solution.py:63
  1239.9 6.2 fusion.90
  1246.3 9.4 reduce-scatter.21.cloned.1.call-done
  1258.8 3.5 copy.51
  1262.3 50.3 %while.27 = (s32[]{:T(128)}, bf16[3,1024,2,64]{1,3,2,0:T(8,128)(2,1)}, bf16[3,1024,2,64]{1,3,2,0:T(8,128)(2,1)}, bf16[3,1024,2,64]{1,3,2,0:T(8,128)(2,1)}, bf16[...) while((s32[]{:T(128)}, ...), condition=%wide.region_25.26_spmd, body=%wide.region_23.25_spmd.sunk | while | flops 1380187136 | bytes 89472296 | solution.py:209
  1268.9 4.1 multiply_reduce_fusion.11
  1273.1 2.7 multiply_convert_fusion.3
  1285.6 4.1 multiply_reduce_fusion.11
  1289.8 2.7 multiply_convert_fusion.3
  1302.3 4.1 multiply_reduce_fusion.11
  1306.5 2.7 multiply_convert_fusion.3
  1319.4 15.9 all-gather.23.cloned.1.call-done
  1335.2 8.9 fusion.91
  1344.2 9.2 fusion.93
  1353.4 9.2 fusion.94
  1364.3 3.5 fusion.95
  1370.5 8.2 all-reduce.1
  1378.8 174.1 %reduce-scatter.23.cloned.1.call-done = f32[768,512]{1,0:T(8,128)} async-done(((f32[6144,512]{1,0:T(8,128)}), f32[768,512]{1,0:T(8,128)}) %reduce-scatter.23.cloned.1.call-update) | async-done | bytes 1572880 | tf_op jit(solution)/shard_map/reduce_scatter | solution.py:82
  1555.1 76.0 %all-reduce = (f32[512]{0:T(512)}, f32[512]{0:T(512)}, f32[512]{0:T(512)}, f32[512]{0:T(512)}, f32[512]{0:T(512)}, /*index=5*/f32[512]{0:T(512)}) all-reduce(f32[512]{0:T(512)S(1)} %get-tuple-element.140, f32[512]{0:T(512)S(1)} %get-tuple-element.145, ...), channel_id=1, replica_groups=mesh['dp'=2,'row'=2,'col'=8] {'dp','col'}, use_global_device_ids=true, to_apply=%region_32.33 | all-reduce | flops 3072 | bytes 24576 | tf_op jit(solution)/shard_map/psum | solution.py:232
  1633.6 3.2 fusion.76
  1636.8 4.5 all-reduce.9.cloned.1.call-done
  (261 shorter events, 109.3 us)
Async XLA Ops:
  7.2 613.4 %copy-start = (bf16[512,512]{1,0:T(8,128)(2,1)S(1)}, bf16[512,512]{1,0:T(8,128)(2,1)}, u32[]{:S(2)}) copy-start(bf16[512,512]{1,0:T(8,128)(2,1)} %param.29) | copy-start | bytes 1572868
  7.2 110.0 %all-gather.9.cloned.1.call-start = ((), (), s32[]{:S(2)}) async-start(), calls=%async_computation.8 | async-start | bytes 7077888 | tf_op jit(solution)/shard_map/all_gather | solution.py:63
  15.8 126.9 %reduce-scatter.9.cloned.1.call-start = ((), (), s32[]{:S(2)}) async-start(), calls=%async_computation.9 | async-start | bytes 14155776 | tf_op jit(solution)/shard_map/reduce_scatter | solution.py:66
  17.0 110.1 %copy-start.11 = (bf16[512,3,128]{0,2,1:T(8,128)(2,1)}, bf16[512,3,128]{0,2,1:T(8,128)(2,1)S(1)}, u32[]{:S(2)}) copy-start(bf16[512,3,128]{0,2,1:T(8,128)(2,1)S(1)} %copy.42) | copy-start | bytes 1179652
  127.1 77.4 %all-gather.11.cloned.1.call-start = ((), (), s32[]{:S(2)}) async-start(), calls=%async_computation.10 | async-start | bytes 2359296 | tf_op jit(solution)/shard_map/all_gather | solution.py:73
  159.4 45.2 %copy-start.22 = (bf16[128,512]{1,0:T(8,128)(2,1)S(1)}, bf16[128,512]{1,0:T(8,128)(2,1)}, u32[]{:S(2)}) copy-start(bf16[128,512]{1,0:T(8,128)(2,1)} %param.25) | copy-start | bytes 393220
  189.7 22.6 %copy-start.4 = (bf16[3,1024,2,64]{1,3,2,0:T(8,128)(2,1)}, bf16[3,1024,2,64]{1,3,2,0:T(8,128)(2,1)S(1)}, u32[]{:S(2)}) copy-start(bf16[3,1024,2,64]{1,3,2,0:T(8,128)(2,1)S(1)} %get-tuple-element.452) | copy-start | bytes 2359300
  189.7 22.6 %copy-start.6 = (bf16[3,1024,2,64]{1,3,2,0:T(8,128)(2,1)}, bf16[3,1024,2,64]{1,3,2,0:T(8,128)(2,1)S(1)}, u32[]{:S(2)}) copy-start(bf16[3,1024,2,64]{1,3,2,0:T(8,128)(2,1)S(1)} %get-tuple-element.453) | copy-start | bytes 2359300
  189.7 22.6 %copy-start.10 = (bf16[3,1024,2,64]{1,3,2,0:T(8,128)(2,1)}, bf16[3,1024,2,64]{1,3,2,0:T(8,128)(2,1)S(1)}, u32[]{:S(2)}) copy-start(bf16[3,1024,2,64]{1,3,2,0:T(8,128)(2,1)S(1)} %get-tuple-element.473) | copy-start | bytes 2359300
  193.3 227.9 %reduce-scatter.11.cloned.1.call-start = ((), (), s32[]{:S(2)}) async-start(), calls=%async_computation.11 | async-start | bytes 14155776 | tf_op jit(solution)/shard_map/reduce_scatter | solution.py:82
  212.4 208.8 %copy-start.2 = (bf16[768,512]{1,0:T(8,128)(2,1)S(1)}, bf16[768,512]{1,0:T(8,128)(2,1)}, u32[]{:S(2)}) copy-start(bf16[768,512]{1,0:T(8,128)(2,1)} %param.19) | copy-start | bytes 2359300
  212.4 308.7 %copy-start.14 = (bf16[512,512]{1,0:T(8,128)(2,1)S(1)}, bf16[512,512]{1,0:T(8,128)(2,1)}, u32[]{:S(2)}) copy-start(bf16[512,512]{1,0:T(8,128)(2,1)} %param.31) | copy-start | bytes 1572868
  212.4 308.6 %all-gather.17.cloned.1.call-start = ((), (), s32[]{:S(2)}) async-start(), calls=%async_computation.16 | async-start | bytes 7077888 | tf_op jit(solution)/shard_map/all_gather | solution.py:63
  213.0 407.6 %all-gather.13.cloned.1.call-start = ((), (), s32[]{:S(2)}) async-start(), calls=%async_computation.12 | async-start | bytes 7077888 | tf_op jit(solution)/shard_map/all_gather | solution.py:63
  425.5 105.0 %copy-start.24 = (f32[768]{0:T(1024)}, f32[768]{0:T(1024)S(1)}, u32[]{:S(2)}) copy-start(f32[768]{0:T(1024)S(1)} %get-tuple-element.150) | copy-start | bytes 9220
  425.5 105.0 %copy-start.26 = (f32[768]{0:T(1024)}, f32[768]{0:T(1024)S(1)}, u32[]{:S(2)}) copy-start(f32[768]{0:T(1024)S(1)} %get-tuple-element.151) | copy-start | bytes 9220
  427.4 214.4 %reduce-scatter.17.cloned.1.call-start = ((), (), s32[]{:S(2)}) async-start(), calls=%async_computation.17 | async-start | bytes 18874368 | tf_op jit(solution)/shard_map/reduce_scatter | solution.py:66
  530.6 136.9 %reduce-scatter.13.cloned.1.call-start = ((), (), s32[]{:S(2)}) async-start(), calls=%async_computation.13 | async-start | bytes 18874368 | tf_op jit(solution)/shard_map/reduce_scatter | solution.py:66
  631.2 65.6 %all-gather.19.cloned.1.call-start = ((), (), s32[]{:S(2)}) async-start(), calls=%async_computation.18 | async-start | bytes 9437184 | tf_op jit(solution)/shard_map/all_gather | solution.py:73
  677.5 38.6 %all-gather.15.cloned.1.call-start = ((), (), s32[]{:S(2)}) async-start(), calls=%async_computation.14 | async-start | bytes 9437184 | tf_op jit(solution)/shard_map/all_gather | solution.py:73
  678.1 250.3 %reduce-scatter.19.cloned.1.call-start = ((), (), s32[]{:S(2)}) async-start(), calls=%async_computation.19 | async-start | bytes 14155776 | tf_op jit(solution)/shard_map/reduce_scatter | solution.py:82
  706.3 432.1 %reduce-scatter.15.cloned.1.call-start = ((), (), s32[]{:S(2)}) async-start(), calls=%async_computation.15 | async-start | bytes 14155776 | tf_op jit(solution)/shard_map/reduce_scatter | solution.py:82
  725.4 203.0 %copy-start.25 = (f32[768]{0:T(1024)S(1)}, f32[768]{0:T(1024)}, u32[]{:S(2)}) copy-start(f32[768]{0:T(1024)} %copy-done.24) | copy-start | bytes 9220
  725.4 203.0 %copy-start.27 = (f32[768]{0:T(1024)S(1)}, f32[768]{0:T(1024)}, u32[]{:S(2)}) copy-start(f32[768]{0:T(1024)} %copy-done.26) | copy-start | bytes 9220
  725.4 203.0 %copy-start.34 = (f32[512]{0:T(512)S(1)}, f32[512]{0:T(512)}, u32[]{:S(2)}) copy-start(f32[512]{0:T(512)} %convert_element_type.98) | copy-start | bytes 6148
  725.4 413.0 %copy-start.13 = (bf16[768,512]{1,0:T(8,128)(2,1)S(1)}, bf16[768,512]{1,0:T(8,128)(2,1)}, u32[]{:S(2)}) copy-start(bf16[768,512]{1,0:T(8,128)(2,1)} %param.33) | copy-start | bytes 2359300
  725.4 514.5 %all-gather.21.cloned.1.call-start = ((), (), s32[]{:S(2)}) async-start(), calls=%async_computation.20 | async-start | bytes 7077888 | tf_op jit(solution)/shard_map/all_gather | solution.py:63
  1142.0 113.7 %reduce-scatter.21.cloned.1.call-start = ((), (), s32[]{:S(2)}) async-start(), calls=%async_computation.21 | async-start | bytes 4718592 | tf_op jit(solution)/shard_map/reduce_scatter | solution.py:66
  1246.2 16.1 copy-start.5
  1246.2 16.1 copy-start.7
  1246.2 89.0 %all-gather.23.cloned.1.call-start = ((), (), s32[]{:S(2)}) async-start(), calls=%async_computation.22 | async-start | bytes 7077888 | tf_op jit(solution)/shard_map/all_gather | solution.py:73
  1316.7 18.5 %copy-start.12 = (bf16[512,3,128]{0,2,1:T(8,128)(2,1)S(1)}, bf16[512,3,128]{0,2,1:T(8,128)(2,1)}, u32[]{:S(2)}) copy-start(bf16[512,3,128]{0,2,1:T(8,128)(2,1)} %copy-done.11) | copy-start | bytes 1179652
  1319.3 233.5 %reduce-scatter.23.cloned.1.call-start = ((), (), s32[]{:S(2)}) async-start(), calls=%async_computation.23 | async-start | bytes 14155776 | tf_op jit(solution)/shard_map/reduce_scatter | solution.py:82
  1344.1 297.2 %all-reduce.9.cloned.1.call-start = ((), (), s32[]{:S(2)}) async-start(), calls=%async_computation.24 | async-start | bytes 6291456 | tf_op jit(solution)/shard_map/psum | solution.py:222
  1344.2 18.4 %slice-start = ((s8[6291456]{0:T(1024)(128)(4,1)}), s8[4194304]{0:T(1024)(128)(4,1)S(1)}, s32[]{:S(2)}) async-start(s8[6291456]{0:T(1024)(128)(4,1)} %bitcast.154), calls=%async_computation.25 | async-start | bytes 8388608
  1344.2 20.1 %slice-start.2 = ((s8[6291456]{0:T(1024)(128)(4,1)}), s8[4194304]{0:T(1024)(128)(4,1)S(1)}, s32[]{:S(2)}) async-start(s8[6291456]{0:T(1024)(128)(4,1)} %bitcast.156), calls=%async_computation.27 | async-start | bytes 8388608
  1344.2 20.1 %slice-start.4 = ((s8[4718592]{0:T(1024)(128)(4,1)}), s8[4194304]{0:T(1024)(128)(4,1)S(1)}, s32[]{:S(2)}) async-start(s8[4718592]{0:T(1024)(128)(4,1)} %bitcast.160), calls=%async_computation.29 | async-start | bytes 8388608
  1353.4 9.2 copy-start.8
  1353.4 10.9 slice-start.3
  1353.4 10.9 slice-start.5
  1367.8 185.0 %copy-start.3 = (bf16[768,512]{1,0:T(8,128)(2,1)S(1)}, bf16[768,512]{1,0:T(8,128)(2,1)}, u32[]{:S(2)}) copy-start(bf16[768,512]{1,0:T(8,128)(2,1)} %param.19) | copy-start | bytes 2359300
  1367.8 185.0 %copy-start.29 = (f32[768]{0:T(1024)S(1)}, f32[768]{0:T(1024)}, u32[]{:S(2)}) copy-start(f32[768]{0:T(1024)} %copy-done.28) | copy-start | bytes 9220
  1367.8 185.0 %copy-start.31 = (f32[768]{0:T(1024)S(1)}, f32[768]{0:T(1024)}, u32[]{:S(2)}) copy-start(f32[768]{0:T(1024)} %copy-done.30) | copy-start | bytes 9220
  1367.8 185.0 %copy-start.33 = (f32[512]{0:T(512)S(1)}, f32[512]{0:T(512)}, u32[]{:S(2)}) copy-start(f32[512]{0:T(512)} %copy-done.32) | copy-start | bytes 6148
  1367.8 187.2 %copy-start.36 = (f32[512]{0:T(512)S(1)}, f32[512]{0:T(512)}, u32[]{:S(2)}) copy-start(f32[512]{0:T(512)} %get-tuple-element.138) | copy-start | bytes 6148
  1367.8 187.2 %copy-start.37 = (f32[512]{0:T(512)S(1)}, f32[512]{0:T(512)}, u32[]{:S(2)}) copy-start(f32[512]{0:T(512)} %get-tuple-element.144) | copy-start | bytes 6148
  1367.9 265.8 %copy-start.9 = (f32[768,512]{1,0:T(8,128)S(1)}, f32[768,512]{1,0:T(8,128)}, u32[]{:S(2)}) copy-start(f32[768,512]{1,0:T(8,128)} %get-tuple-element.214) | copy-start | bytes 4718596
  1633.6 14.7 copy-start.1
  (31 other events, 72.2 us)
Sparse Core Ops, SparseCore 0:
  15.9 101.2 all-gather.8
  127.2 15.3 reduce-scatter.8
  193.4 11.0 all-gather.10
  212.5 208.6 reduce-scatter.10
  423.2 97.7 all-gather.16
  523.7 96.8 all-gather.12
  622.9 18.9 reduce-scatter.16
  644.1 23.3 reduce-scatter.12
  677.6 19.1 all-gather.18
  698.2 17.9 all-gather.14
  719.8 208.5 reduce-scatter.18
  931.8 206.5 reduce-scatter.14
  1142.1 97.7 all-gather.20
  1246.3 9.3 reduce-scatter.20
  1319.4 15.7 all-gather.22
  1344.2 208.5 reduce-scatter.22
  1556.3 84.9 all-reduce.8
where the time goes:
time: 1660 us
  waiting for transfers between devices  1290 us (78%)
  matrix products  142 us (9%)
  blocking collectives  94.5 us (6%)
  other arithmetic  67 us (4%)
  local copies, waits for them, and re-layouts  45.4 us (3%)
    reduce_scatter x4, waiting for transfers between devices, row_then_col(): lax.psum_scatter(product(block_rows, weight, flipped), 'col', scatter_dim...  787 us
    all_gather x4, waiting for transfers between devices, col_then_row(): gathered = lax.all_gather(shard_in, 'col', axis=0, tiled=True)  382 us
    psum x1, blocking collectives, per_device(): lax.psum((grad_attend_gain, grad_attend_shift, grad_output_bias, grad_fee...  76 us
    reduce_scatter x4, waiting for transfers between devices, col_then_row(): lax.psum_scatter(product(gathered, weight, flipped), 'row', scatter_dimen...  59.9 us
    all_gather x4, waiting for transfers between devices, row_then_col(): lax.all_gather(for_sending(shard_in), 'row', axis=0, tiled=True)  55.5 us
    dot_general x4, matrix products, product(): return jnp.dot(left_side, right_side, preferred_element_type=jnp.float32)  37.4 us
    dot_general x4, matrix products, product(): lax.dot_general(left_side, right_side, (((1,), (1,)), ((), ())), preferre...  34.1 us
  transfers between devices with their start and end apart: 17, of which 17 were waited for; matrix products, arithmetic and copies ran while one was open for 5% of the time, Pallas kernels for 0%

commit v1 on v0

v1 whole, which is shorter than its diff:
```python
import math
from functools import partial

import jax
import jax.numpy as jnp
from jax import lax
from jax.experimental import pallas as pl
from jax.experimental.pallas import tpu as pltpu
from jax.sharding import PartitionSpec as P

HD = 64

epsilon = 1e-05
masked_score = -1000000000.0
low = jnp.bfloat16
full = jnp.float32


def dot_nn(left, right):
    return lax.dot_general(left, right, (((1,), (0,)), ((), ())), preferred_element_type=full)


def dot_nt(left, right):
    return lax.dot_general(left, right, (((1,), (1,)), ((), ())), preferred_element_type=full)


def dot_tn(left, right):
    return lax.dot_general(left, right, (((0,), (0,)), ((), ())), preferred_element_type=full)


def ring_order(count):
    across = {8: 2, 16: 4}.get(count, 1)
    along = count // across
    order = [z * across for z in range(along)]
    for step in range(along):
        z = along - 1 - step
        turn = range(1, across) if step % 2 == 0 else range(across - 1, 0, -1)
        order += [z * across + y for y in turn]
    return order


def shift(values, count, backward):
    order = ring_order(count)
    pairs = [(order[i], order[(i + 1) % count]) for i in range(count)]
    if backward:
        pairs = [(b, a) for a, b in pairs]
    return lax.ppermute(values, "col", pairs)


def ring_gather(ahead, behind, count):
    ahead, behind = [ahead], [behind]
    for _ in range(count - 1):
        ahead.append(shift(ahead[-1], count, False))
        behind.append(shift(behind[-1], count, True))
    return ahead, behind


def ring_scatter(ahead, behind, count):
    one, two = ahead[1 % count].astype(low), behind[1 % count].astype(low)
    for step in range(1, count):
        later = (step + 1) % count
        one = (shift(one, count, False).astype(full) + ahead[later].astype(full)).astype(low)
        two = (shift(two, count, True).astype(full) + behind[later].astype(full)).astype(low)
    return one, two


def swap(values):
    return lax.ppermute(values, "row", [(0, 1), (1, 0)])


def forward_kernel(
    blk, own, low_ref, proj_ref, key_ids, query_ids, out_ref, lse_ref, keys, peak, total, acc
):
    i = pl.program_id(1)

    @pl.when(i == 0)
    def _():
        keys[...] = jnp.transpose(proj_ref[HD : 2 * HD, :])

    start = pl.multiple_of(own + i * blk, blk)
    queries = proj_ref[0:HD, pl.ds(start, blk)] * jnp.asarray(HD**-0.5, low)
    ids = query_ids[...]

    def scores_of(at):
        same = key_ids[pl.ds(at, blk), :] == ids
        return dot_nn(keys[pl.ds(at, blk), :], queries), same

    scores, same = scores_of(start)
    rows = lax.broadcasted_iota(jnp.int32, (blk, blk), 0)
    columns = lax.broadcasted_iota(jnp.int32, (blk, blk), 1)
    scores = jnp.where(same & (rows <= columns), scores, masked_score)
    highest = jnp.max(scores, axis=0, keepdims=True)
    weights = jnp.exp(scores - highest)
    peak[...] = highest
    total[...] = jnp.sum(weights, axis=0, keepdims=True)
    acc[...] = dot_nn(proj_ref[2 * HD : 3 * HD, pl.ds(start, blk)], weights.astype(low))

    def body(j, carry):
        at = pl.multiple_of(j * blk, blk)
        scores, same = scores_of(at)
        scores = jnp.where(same, scores, masked_score)
        before = peak[...]
        highest = jnp.maximum(before, jnp.max(scores, axis=0, keepdims=True))
        shrink = jnp.exp(before - highest)
        weights = jnp.exp(scores - highest)
        peak[...] = highest
        total[...] = total[...] * shrink + jnp.sum(weights, axis=0, keepdims=True)
        acc[...] = acc[...] * shrink + dot_nn(
            proj_ref[2 * HD : 3 * HD, pl.ds(at, blk)], weights.astype(low)
        )
        return carry

    lax.fori_loop(low_ref[i], own // blk + i, body, 0)
    out_ref[...] = (acc[...] / total[...]).astype(low)
    lse_ref[...] = jnp.broadcast_to(peak[...] + jnp.log(total[...]), lse_ref.shape)


def backward_kernel(
    blk,
    own,
    low_ref,
    proj_ref,
    key_ids,
    query_ids,
    out_ref,
    lse_ref,
    grad_ref,
    grad_proj,
    keys,
    values,
    grad_keys,
    grad_values,
    grad_queries,
):
    i = pl.program_id(1)

    @pl.when(i == 0)
    def _():
        keys[...] = jnp.transpose(proj_ref[HD : 2 * HD, :])
        values[...] = jnp.transpose(proj_ref[2 * HD : 3 * HD, :])
        grad_keys[...] = jnp.zeros_like(grad_keys)
        grad_values[...] = jnp.zeros_like(grad_values)
        grad_proj[0:HD, 0:own] = jnp.zeros((HD, own), low)

    start = pl.multiple_of(own + i * blk, blk)
    scaling = jnp.asarray(HD**-0.5, low)
    queries = proj_ref[0:HD, pl.ds(start, blk)] * scaling
    ids = query_ids[...]
    summary = lse_ref[0:1, :]
    grad_out = grad_ref[...]
    against = jnp.sum(
        out_ref[...].astype(full) * grad_out.astype(full), axis=0, keepdims=True
    )

    def block(at, diagonal):
        same = key_ids[pl.ds(at, blk), :] == ids
        if diagonal:
            rows = lax.broadcasted_iota(jnp.int32, (blk, blk), 0)
            columns = lax.broadcasted_iota(jnp.int32, (blk, blk), 1)
            same = same & (rows <= columns)
        scores = dot_nn(keys[pl.ds(at, blk), :], queries)
        chances = jnp.exp(jnp.where(same, scores, masked_score) - summary)
        grad_chances = dot_nn(values[pl.ds(at, blk), :], grad_out)
        grad_values[:, pl.ds(at, blk)] += dot_nt(grad_out, chances.astype(low))
        grad_scores = (chances * (grad_chances - against)).astype(low)
        grad_keys[:, pl.ds(at, blk)] += dot_nt(queries, grad_scores)
        return dot_nn(proj_ref[HD : 2 * HD, pl.ds(at, blk)], grad_scores)

    grad_queries[...] = block(start, True)

    def body(j, carry):
        grad_queries[...] += block(pl.multiple_of(j * blk, blk), False)
        return carry

    lax.fori_loop(low_ref[i], own // blk + i, body, 0)
    grad_proj[0:HD, pl.ds(start, blk)] = (grad_queries[...] * (HD**-0.5)).astype(low)

    @pl.when(i == pl.num_programs(1) - 1)
    def _():
        grad_proj[HD : 2 * HD, :] = grad_keys[...].astype(low)
        grad_proj[2 * HD : 3 * HD, :] = grad_values[...].astype(low)


def attention_specs(blk, own, seen):
    proj = pl.BlockSpec((3 * HD, seen), lambda h, i, s: (h, 0))
    key_ids = pl.BlockSpec((seen, 1), lambda h, i, s: (0, 0))
    query_ids = pl.BlockSpec((1, blk), lambda h, i, s: (0, i))
    out = pl.BlockSpec((HD, blk), lambda h, i, s: (h, i))
    lse = pl.BlockSpec((8, blk), lambda h, i, s: (h, i))
    return proj, key_ids, query_ids, out, lse


def attend_forward(proj, lows, key_ids, query_ids, blk):
    heads, seen = proj.shape[0] // (3 * HD), proj.shape[1]
    own = query_ids.shape[1]
    proj_spec, key_spec, query_spec, out_spec, lse_spec = attention_specs(blk, own, seen)
    return pl.pallas_call(
        partial(forward_kernel, blk, seen - own),
        out_shape=(
            jax.ShapeDtypeStruct((heads * HD, own), low),
            jax.ShapeDtypeStruct((heads * 8, own), full),
        ),
        grid_spec=pltpu.PrefetchScalarGridSpec(
            num_scalar_prefetch=1,
            grid=(heads, own // blk),
            in_specs=[proj_spec, key_spec, query_spec],
            out_specs=[out_spec, lse_spec],
            scratch_shapes=[
                pltpu.VMEM((seen, HD), low),
                pltpu.VMEM((1, blk), full),
                pltpu.VMEM((1, blk), full),
                pltpu.VMEM((HD, blk), full),
            ],
        ),
        cost_estimate=pl.CostEstimate(
            flops=heads * own * 1024 * HD * 8,
            bytes_accessed=heads * HD * seen * 8,
            transcendentals=heads * own * 512,
        ),
        name="attend_forward",
    )(lows, proj, key_ids, query_ids)


def attend_backward(proj, lows, key_ids, query_ids, out, lse, grad, blk):
    heads, seen = proj.shape[0] // (3 * HD), proj.shape[1]
    own = query_ids.shape[1]
    proj_spec, key_spec, query_spec, out_spec, lse_spec = attention_specs(blk, own, seen)
    return pl.pallas_call(
        partial(backward_kernel, blk, seen - own),
        out_shape=jax.ShapeDtypeStruct(proj.shape, low),
        grid_spec=pltpu.PrefetchScalarGridSpec(
            num_scalar_prefetch=1,
            grid=(heads, own // blk),
            in_specs=[proj_spec, key_spec, query_spec, out_spec, lse_spec, out_spec],
            out_specs=proj_spec,
            scratch_shapes=[
                pltpu.VMEM((seen, HD), low),
                pltpu.VMEM((seen, HD), low),
                pltpu.VMEM((HD, seen), full),
                pltpu.VMEM((HD, seen), full),
                pltpu.VMEM((HD, blk), full),
            ],
        ),
        cost_estimate=pl.CostEstimate(
            flops=heads * own * 1024 * HD * 16,
            bytes_accessed=heads * HD * seen * 16,
            transcendentals=heads * own * 512,
        ),
        name="attend_backward",
    )(lows, proj, key_ids, query_ids, out, lse, grad)


def norm_forward(values):
    average = jnp.mean(values, axis=1, keepdims=True)
    square = jnp.mean(values * values, axis=1, keepdims=True)
    inverse = lax.rsqrt(square - average * average + epsilon)
    return (values - average) * inverse, inverse


def halves(array):
    middle = array.shape[0] // 2
    return array[:middle], array[middle:]


def per_device(
    tokens,
    segments,
    attend_gain,
    attend_shift,
    input_weight,
    input_bias,
    output_weight,
    output_bias,
    feed_gain,
    feed_shift,
    up_weight,
    up_bias,
    down_weight,
    down_bias,
    grad_out,
):
    row, col = lax.axis_index("row"), lax.axis_index("col")
    count = lax.axis_size("col")
    own, half = tokens.shape
    length = segments.shape[1]
    blk = min(256, math.gcd(own, length))
    head_width = input_weight.shape[2]
    split_heads = head_width % (2 * HD) == 0
    hidden_width = up_weight.shape[1]
    first_core = row == 0

    def to_core(block):
        one, two = halves(block)
        kept = jnp.where(first_core, one, two)
        sent = jnp.where(first_core, two, one)
        return jnp.concatenate([kept, swap(sent)], axis=1)

    def from_core(block):
        kept, got = block[:, :half], swap(block[:, half:])
        one = jnp.where(first_core, kept, got)
        two = jnp.where(first_core, got, kept)
        return jnp.concatenate([one, two], axis=0)

    def from_other(block):
        block = block.astype(low)
        return swap(jnp.concatenate([block[:, half:], block[:, :half]], axis=1)).astype(full)

    def over_dp(block):
        if lax.axis_size("dp") == 2:
            other = lax.ppermute(block.astype(low), "dp", [(0, 1), (1, 0)])
            return block.astype(low).astype(full) + other.astype(full)
        return lax.psum(block.astype(full), "dp")

    vectors = jnp.stack(
        [attend_gain, attend_shift, output_bias, feed_gain, feed_shift, down_bias]
    )
    vectors = jnp.concatenate([vectors, swap(vectors)], axis=1).astype(full)
    gain_one, shift_one, out_bias, gain_two, shift_two, _ = [vectors[k : k + 1] for k in range(6)]

    needs = [c for c in range(count) if (c * own) % length != 0]
    assert all((c * own) % length <= own for c in needs)
    halo = lax.ppermute(tokens, "col", [(c - 1, c) for c in needs])
    x_own = jnp.concatenate([tokens, swap(tokens)], axis=1).astype(full)
    x_halo = jnp.concatenate([halo, swap(halo)], axis=1).astype(full)

    other_labels = swap(segments)
    labels = jnp.concatenate(
        [
            jnp.where(first_core, segments, other_labels),
            jnp.where(first_core, other_labels, segments),
        ],
        axis=0,
    ).reshape(-1)
    places = jnp.arange(labels.shape[0], dtype=jnp.int32)
    idents = jnp.where(labels > 0, (places // length) * 4096 + labels, -1 - places)
    idents = jnp.concatenate([jnp.full((own,), -(2**30), jnp.int32), idents])
    idents = lax.dynamic_slice_in_dim(idents, col * own, 2 * own, 0)
    key_ids = idents[:, None]
    query_ids = idents[None, own:]
    heads_of_blocks = idents[own::blk]
    lows = jnp.argmax(idents[None, :] == heads_of_blocks[:, None], axis=1).astype(jnp.int32) // blk

    in_block = jnp.transpose(input_weight, (2, 1, 0))
    if split_heads:
        in_block = in_block.reshape(head_width // HD, HD, 3, half).transpose(0, 2, 1, 3)
        in_block = in_block.reshape(3 * head_width, half)
        bias_in = input_bias.reshape(2, head_width // HD, HD)
        bias_in = jnp.stack([bias_in[0], jnp.zeros_like(bias_in[0]), bias_in[1]], axis=1)
        one, two = halves(bias_in.reshape(-1))
        bias_in = jnp.where(first_core, one, two)
        in_block = to_core(in_block)
        out_block = to_core(output_weight)
    up_block = to_core(jnp.transpose(up_weight))
    down_block = to_core(down_weight)
    one, two = halves(up_bias)
    bias_up = jnp.where(first_core, one, two)

    def as_rows(vector):
        return jnp.pad(vector[None, :], ((0, 15), (0, 2 * half - vector.shape[0])))

    def join(ahead, behind):
        parts = []
        for t in range(count):
            parts += [ahead[t], behind[(count - t) % count]]
        return jnp.concatenate(parts, axis=0)

    def part(block, unit):
        mid = unit // 2
        ahead = [block[t * unit : t * unit + mid] for t in range(count)]
        behind = [None] * count
        for t in range(count):
            behind[(count - t) % count] = block[t * unit + mid : (t + 1) * unit]
        return ahead, behind

    up_width = up_block.shape[0]
    extra = [bias_up]
    if split_heads:
        in_width, out_width = in_block.shape[0], out_block.shape[0]
        extra = [bias_in, bias_up]
        packed = [halves(in_block), halves(out_block)]
    else:
        packed = []
    extra = [halves(v) for v in extra]
    packed.append([as_rows(jnp.concatenate([v[k] for v in extra])) for k in range(2)])
    sizes = [p[0].shape[0] for p in packed]
    ahead, behind = ring_gather(
        jnp.concatenate([p[0] for p in packed]), jnp.concatenate([p[1] for p in packed]), count
    )
    groups, at = [], 0
    for size in sizes:
        groups.append(join([a[at : at + size] for a in ahead], [b[at : at + size] for b in behind]))
        at += size
    bias_rows = groups[-1].reshape(2 * count, 16, 2 * half)[:, 0]
    if split_heads:
        in_all, out_all = groups[0], groups[1]
        mid = in_width // 2
        bias_in_all = bias_rows[:, :mid].reshape(-1, 1).astype(full)
        bias_up_all = bias_rows[:, mid : mid + up_width // 2].reshape(1, -1).astype(full)
    else:
        bias_up_all = bias_rows[:, : up_width // 2].reshape(1, -1).astype(full)
        heads = count * head_width // HD
        gathered = lax.all_gather(in_block, "col", axis=0, tiled=True)
        gathered = gathered.reshape(heads, HD, 3, half).transpose(0, 2, 1, 3)
        in_all = to_core(gathered.reshape(heads * 3 * HD, half))
        out_all = to_core(lax.all_gather(output_weight, "col", axis=0, tiled=True))
        bias_all = lax.all_gather(input_bias, "col", axis=1, tiled=True).reshape(2, heads, HD)
        bias_all = jnp.stack([bias_all[0], jnp.zeros_like(bias_all[0]), bias_all[1]], axis=1)
        one, two = halves(bias_all.reshape(-1, 1).astype(full))
        bias_in_all = jnp.where(first_core, one, two)
    up_all = join(*ring_gather(*halves(up_block), count))
    down_all = join(*ring_gather(*halves(down_block), count))

    normed_one, inverse_one = norm_forward(x_own)
    normed_halo, _ = norm_forward(x_halo)
    first = jnp.concatenate([normed_halo, normed_one]) * gain_one + shift_one
    first = first.astype(low)
    proj = (dot_nt(in_all, first) + bias_in_all).astype(low)
    attended, lse = attend_forward(proj, lows, key_ids, query_ids, blk)
    branch = dot_tn(attended, out_all)
    middle = x_own + (branch + from_other(branch) + out_bias)
    normed_two, inverse_two = norm_forward(middle)
    second = (normed_two * gain_two + shift_two).astype(low)
    hidden_pre = dot_nt(second, up_all) + bias_up_all
    gelu_tanh = partial(jax.nn.gelu, approximate=True)
    hidden = gelu_tanh(hidden_pre).astype(low)
    branch = dot_nn(hidden, down_all)
    branch = branch[:, :half] + swap(branch[:, half:].astype(low)).astype(full)
    layer_out = (middle[:, :half] + (branch + down_bias.astype(full))).astype(low)

    grad_full = jnp.concatenate([grad_out, swap(grad_out)], axis=1)
    grad_top = grad_full.astype(full)
    grad_down_bias = jnp.sum(grad_out.astype(full), axis=0)
    grad_down = dot_tn(hidden, grad_full)
    grad_hidden = dot_nt(grad_full, down_all)
    _, gelu_pull = jax.vjp(gelu_tanh, hidden_pre)
    grad_pre = gelu_pull(grad_hidden)[0].astype(low)
    grad_up_bias = jnp.sum(grad_pre.astype(full), axis=0)
    grad_second = dot_nn(grad_pre, up_all)
    grad_up = dot_tn(grad_pre, second)
    grad_second = grad_second + from_other(grad_second)
    scaled = grad_second * gain_two
    grad_middle = grad_top + inverse_two * (
        scaled
        - jnp.mean(scaled, axis=1, keepdims=True)
        - normed_two * jnp.mean(scaled * normed_two, axis=1, keepdims=True)
    )
    grad_feed_gain = jnp.sum(grad_second[:, :half] * normed_two[:, :half], axis=0)
    grad_feed_shift = jnp.sum(grad_second[:, :half], axis=0)
    grad_branch = grad_middle.astype(low)
    grad_output_bias = jnp.sum(grad_branch[:, :half].astype(full), axis=0)
    grad_attended = dot_nt(out_all, grad_branch).astype(low)
    grad_output = dot_nn(attended, grad_branch)
    grad_proj = attend_backward(
        proj, lows, key_ids, query_ids, attended, lse, grad_attended, blk
    )
    grad_bias_in = jnp.sum(grad_proj.astype(full), axis=1)
    grad_input = dot_nn(grad_proj, first)
    grad_first = dot_tn(grad_proj, in_all)
    grad_first = grad_first[:, :half] + swap(grad_first[:, half:].astype(low)).astype(full)
    returned = lax.ppermute(grad_first[:own].astype(low), "col", [(c, c - 1) for c in needs])
    grad_first = grad_first[own:] + returned.astype(full)
    scaled = grad_first * gain_one[:, :half]
    normed_own = normed_one[:, :half]
    sums = jnp.concatenate(
        [
            jnp.sum(scaled, axis=1, keepdims=True),
            jnp.sum(scaled * normed_own, axis=1, keepdims=True),
        ],
        axis=1,
    )
    sums = (sums + swap(sums)) / (2 * half)
    grad_tokens = grad_middle[:, :half] + inverse_one * (
        scaled - sums[:, 0:1] - normed_own * sums[:, 1:2]
    )
    grad_attend_gain = jnp.sum(grad_first * normed_own, axis=0)
    grad_attend_shift = jnp.sum(grad_first, axis=0)

    def finish(one, two):
        return over_dp(from_core(jnp.concatenate([one, two], axis=0)))

    def both(one, two):
        return jnp.concatenate([one, two], axis=0)

    grad_down_weight = finish(*ring_scatter(*part(grad_down, up_width), count))
    grad_up_weight = jnp.transpose(finish(*ring_scatter(*part(grad_up, up_width), count)))

    sum_up = grad_up_bias.reshape(2 * count, up_width // 2)
    if split_heads:
        sum_in = grad_bias_in.reshape(2 * count, in_width // 2)
        sums_rows = jnp.concatenate([sum_in, sum_up], axis=1)
    else:
        sums_rows = sum_up
    used = sums_rows.shape[1]
    sums_rows = jnp.pad(sums_rows[:, None, :], ((0, 0), (0, 15), (0, 2 * half - used)))
    sums_rows = sums_rows.reshape(2 * count * 16, 2 * half)
    parts = [part(sums_rows, 32)]
    if split_heads:
        parts = [part(grad_input, in_width), part(grad_output, out_width)] + parts
    ahead = [jnp.concatenate([p[0][t] for p in parts]) for t in range(count)]
    behind = [jnp.concatenate([p[1][t] for p in parts]) for t in range(count)]
    one, two = ring_scatter(ahead, behind, count)
    pieces, at = [], 0
    for size in sizes:
        pieces.append(jnp.concatenate([one[at : at + size], two[at : at + size]]))
        at += size
    bias_sums = jnp.concatenate([pieces[-1][0:1], pieces[-1][16:17]])
    if split_heads:
        joined = over_dp(from_core(jnp.concatenate(pieces[:2], axis=0)))
        per_core = joined.reshape(2, in_width + out_width, half)
        grad_in = per_core[:, :in_width].reshape(head_width // HD, 3, HD, half)
        grad_input_weight = grad_in.transpose(3, 1, 0, 2).reshape(half, 3, head_width)
        grad_output_weight = per_core[:, in_width:].reshape(head_width, half)
        mid = in_width // 2
        mine_in = bias_sums[:, :mid].reshape(-1)
        mine_up = bias_sums[:, mid : mid + up_width // 2].reshape(-1)
        mine = jnp.concatenate([mine_in, mine_up])
    else:
        heads = count * head_width // HD
        grad_in = from_core(grad_input.astype(low)).reshape(heads, 3, HD, half)
        grad_in = grad_in.transpose(0, 2, 1, 3).reshape(heads * HD, 3, half).astype(full)
        grad_in = lax.psum_scatter(grad_in, "col", scatter_dimension=0, tiled=True)
        grad_input_weight = over_dp(grad_in).transpose(2, 1, 0)
        grad_output_weight = from_core(grad_output.astype(low)).astype(full)
        grad_output_weight = lax.psum_scatter(
            grad_output_weight, "col", scatter_dimension=0, tiled=True
        )
        grad_output_weight = over_dp(grad_output_weight)
        mine = bias_sums[:, : up_width // 2].reshape(-1)
    other = swap(mine)
    mine = over_dp(
        jnp.stack([jnp.where(first_core, mine, other), jnp.where(first_core, other, mine)])
    )
    grad_up_bias = mine[:, -up_width:].reshape(-1)
    if split_heads:
        bias = mine[:, :in_width].reshape(head_width // HD, 3, HD)
        grad_input_bias = jnp.stack([bias[:, 0].reshape(-1), bias[:, 2].reshape(-1)])
    else:
        bias = grad_bias_in.reshape(heads // 2, 3, HD)
        bias = jnp.stack([bias[:, 0].reshape(-1), bias[:, 2].reshape(-1)])
        other = swap(bias)
        bias = jnp.concatenate(
            [jnp.where(first_core, bias, other), jnp.where(first_core, other, bias)], axis=1
        )
        bias = lax.psum_scatter(bias, "col", scatter_dimension=1, tiled=True)
        grad_input_bias = lax.psum(bias, "dp")

    small = jnp.stack(
        [
            grad_attend_gain,
            grad_attend_shift,
            grad_output_bias,
            grad_feed_gain,
            grad_feed_shift,
            grad_down_bias,
        ]
    )
    small = lax.psum(small, ("dp", "col"))
    return (
        layer_out,
        grad_tokens,
        small[0],
        small[1],
        grad_input_weight,
        grad_input_bias,
        grad_output_weight,
        small[2],
        small[3],
        small[4],
        grad_up_weight,
        grad_up_bias,
        grad_down_weight,
        small[5],
    )


def solution(mesh):
    in_specs = (
        P(("dp", "col"), "row"),
        P(("dp", "row"), None),
        P("row"),
        P("row"),
        P("row", None, "col"),
        P(None, "col"),
        P("col", "row"),
        P("row"),
        P("row"),
        P("row"),
        P("row", "col"),
        P("col"),
        P("col", "row"),
        P("row"),
        P(("dp", "col"), "row"),
    )
    out_specs = (
        P(("dp", "col"), "row"),
        P(("dp", "col"), "row"),
        P("row"),
        P("row"),
        P("row", None, "col"),
        P(None, "col"),
        P("col", "row"),
        P("row"),
        P("row"),
        P("row"),
        P("row", "col"),
        P("col"),
        P("col", "row"),
        P("row"),
    )
    return jax.shard_map(
        per_device, mesh=mesh, in_specs=in_specs, out_specs=out_specs, check_vma=False
    )
```

time: 1660 us -> 655 us (0.39)
  waiting for transfers between devices: 1290 us -> 168 us
  starting transfers between devices: 1.28 us -> 127 us
  matrix products: 142 us -> 76.3 us
  Pallas kernels: 0 us -> 46.3 us
  local copies, waits for them, and re-layouts: 45.4 us -> 89.3 us
  blocking collectives: 94.5 us -> 73.4 us
    reduce_scatter x8 -> x0, waiting for transfers between devices: 847 us -> none  [the longest x4 787 us: row_then_col(): lax.psum_scatter(product(block_rows, weight, flipped), 'col', scatter_dim...]
    all_gather x8 -> x0, waiting for transfers between devices: 437 us -> none  [the longest x4 382 us: col_then_row(): gathered = lax.all_gather(shard_in, 'col', axis=0, tiled=True)]
    ppermute x0 -> x108, waiting for transfers between devices: none -> 168 us  [the longest x84 157 us: shift(): return lax.ppermute(values, 'col', pairs)]
    ppermute x0 -> x108, starting transfers between devices: none -> 127 us  [the longest x84 117 us: shift(): return lax.ppermute(values, 'col', pairs)]
    dot_general x33 -> x12, matrix products: 142 us -> 76.3 us  [the longest x4 31.6 us: dot_tn(): lax.dot_general(left, right, (((0,), (0,)), ((), ())), preferred_element_...]
    unnamed x95 -> x265, local copies, waits for them, and re-layouts: 14.4 us -> 63.3 us
    pallas_call x0 -> x2, Pallas kernels: none -> 46.3 us  [the longest x1 24.2 us: attend_backward(): pl.pallas_call(partial(backward_kernel, blk, seen - own), out_shape=jax.S...]
    reduce_sum x10 -> x9, other arithmetic: 29.8 us -> 7.29 us  [the longest x3 2.03 us: norm_forward(): average = jnp.mean(values, axis=1, keepdims=True)]
  transfers between devices with their start and end apart: 17 -> 108, of which waited for: 17 -> 51; matrix products, arithmetic and copies ran while one was open for 5% -> 26% of each run, Pallas kernels for 0% -> 7%
where the time goes in v1:
time: 655 us; the launch traced here: 645 us
  waiting for transfers between devices  168 us (26%)
  starting transfers between devices  127 us (19%)
  local copies, waits for them, and re-layouts  89.3 us (14%)
  matrix products  76.3 us (12%)
  blocking collectives  73.4 us (11%)
  other arithmetic  61.6 us (9%)
  Pallas kernels  46.3 us (7%)
    ppermute x84, waiting for transfers between devices, shift(): return lax.ppermute(values, 'col', pairs)  157 us
    ppermute x84, starting transfers between devices, shift(): return lax.ppermute(values, 'col', pairs)  117 us
    psum x1, blocking collectives, per_device(): small = lax.psum(small, ('dp', 'col'))  73.4 us
    unnamed x265, local copies, waits for them, and re-layouts  63.3 us
    dot_general x4, matrix products, dot_tn(): lax.dot_general(left, right, (((0,), (0,)), ((), ())), preferred_element_...  31.6 us
    pallas_call x1, Pallas kernels, attend_backward(): pl.pallas_call(partial(backward_kernel, blk, seen - own), out_shape=jax.S...  24.2 us
    dot_general x4, matrix products, dot_nt(): lax.dot_general(left, right, (((1,), (1,)), ((), ())), preferred_element_...  24 us
    pallas_call x1, Pallas kernels, attend_forward(): pl.pallas_call(partial(forward_kernel, blk, seen - own), out_shape=(jax.S...  22.2 us
  transfers between devices with their start and end apart: 108, of which 51 were waited for; matrix products, arithmetic and copies ran while one was open for 26% of the time, Pallas kernels for 7%

profile of v1, /device:TPU:0, one launch (start us, length us, event | category | flops | bytes accessed | tf_op | source)
XLA Modules:
  0.0 645.1 jit_solution(8999269629498129983)
XLA Ops:
  23.1 3.0 collective-permute-start.4
  39.6 4.0 collective-permute-start.18
  51.0 16.3 %collective-permute-done.40 = bf16[128,1024]{1,0:T(8,128)(2,1)S(1)} collective-permute-done((bf16[128,1024]{1,0:T(8,128)(2,1)S(1)}, bf16[128,1024]{1,0:T(8,128)(2,1)S(1)}, u32[]{:S(2)}, u32[]{:S(2)}) %collective-permute-start.40) | collective-permute-done | bytes 262176 | tf_op jit(solution)/shard_map/ppermute | solution.py:47
  74.7 2.7 collective-permute-done.31
  83.5 3.8 collective-permute-done.6
  89.4 3.6 collective-permute-done.41
  95.1 3.6 collective-permute-done.26
  101.6 3.3 collective-permute-done.7
  107.0 3.5 collective-permute-done.42
  113.2 3.0 collective-permute-done.27
  118.3 4.2 collective-permute-done.8
  125.0 3.1 collective-permute-done.43
  130.1 3.6 collective-permute-done.28
  142.1 3.6 collective-permute-done.44
  153.3 4.3 collective-permute-done.10
  159.7 3.6 collective-permute-done.45
  165.8 3.0 collective-permute-done.30
  169.6 3.0 collective-permute-done.11
  200.3 8.9 %add_convert_fusion.proj_ref = bf16[1536,1536]{1,0:T(8,128)(2,1)} fusion(bf16[1536,1024]{1,0:T(8,128)(2,1)} %slice_dynamic-update-slice_fusion, f32[1536]{0:T(1024)S(1)} %reshape.201, f32[768,1024]{1,0:T(8,128)S(1)} %fusion.11, f32[768,1024]{1,0:T(8,128)S(1)} %copy-done.16, f32[1024]{0:T(1024)S(1)} %bitcast.125, f32[1024]{0:T(1024)S(1)} %bitcast.127), kind=kOutput, calls=%fused_computation.1 | convolution fusion | flops 4842848256 | bytes 14170112 | tf_op jit(solution)/shard_map/dot_general | solution.py:24
  209.2 22.2 %attend_forward.1 = (bf16[512,768]{1,0:T(8,128)(2,1)}, f32[64,768]{1,0:T(8,128)}) custom-call(s32[3]{0:T(128)} %and_select_fusion.low_ref, bf16[1536,1536]{1,0:T(8,128)(2,1)} %add_convert_fusion.proj_ref, s32[1536,1]{1,0:T(8,128)} %broadcast_in_dim.40.key_ids, s32[1,768]{1,0:T(1,128)} %broadcast_in_dim.17.query_ids), custom_call_target="tpu_custom_call" | custom-call | flops 3221225472 | bytes 6291456 | tf_op jit(solution)/shard_map/attend_forward/pallas_call | solution.py:197
  258.8 3.5 fusion.62
  264.9 5.8 fusion.103
  270.7 9.7 %convert_reduce_fusion.1 = (f32[2048]{0:T(1024)S(1)}, bf16[768,2048]{1,0:T(8,128)(2,1)S(1)}) fusion(f32[768,2048]{1,0:T(8,128)} %copy-done.94, f32[2048]{0:T(1024)S(1)} %fusion.94, bf16[768,1024]{1,0:T(8,128)(2,1)S(1)} %copy-done.15, bf16[2048,1024]{1,0:T(8,128)(2,1)S(1)} %copy-done.75), kind=kOutput, calls=%fused_computation.29 | convolution fusion | flops 3257399296 | bytes 15220736 | tf_op jit(solution)/shard_map/dot_general | solution.py:24
  280.4 4.6 fusion.119
  284.9 6.3 fusion.122
  291.3 12.8 %fusion.123 = (bf16[2048,1024]{1,0:T(8,128)(2,1)}, f32[2048,1024]{1,0:T(8,128)S(1)}) fusion(bf16[768,1024]{1,0:T(8,128)(2,1)S(1)} %copy-done.15, f32[768,2048]{1,0:T(8,128)} %copy-done.94, f32[2048]{0:T(1024)S(1)} %fusion.94), kind=kOutput, calls=%fused_computation.399 | convolution fusion | flops 3239051264 | bytes 20455424 | tf_op jit(solution)/shard_map/dot_general | solution.py:28
  310.0 13.8 %collective-permute-start.76 = (bf16[128,1024]{1,0:T(8,128)(2,1)S(1)}, bf16[128,1024]{1,0:T(8,128)(2,1)S(1)}, u32[]{:S(2)}, u32[]{:S(2)}) collective-permute-start(bf16[128,1024]{1,0:T(8,128)(2,1)S(1)} %get-tuple-element.146), channel_id=1, source_target_pairs={{0,2},{2,4},{4,6},{6,7},{7,5},{5,3},{3,1},{1,0},{8,10},{10,12},{12... | collective-permute-start | bytes 786440 | tf_op jit(solution)/shard_map/ppermute | solution.py:47
  327.3 3.2 collective-permute-done.76
  333.2 2.9 collective-permute-done.92
  353.0 4.0 collective-permute-done.85
  359.2 3.4 collective-permute-done.101
  389.4 2.7 fusion.106
  394.7 24.2 %attend_backward.1 = bf16[1536,1536]{1,0:T(8,128)(2,1)} custom-call(s32[3]{0:T(128)} %and_select_fusion.low_ref, bf16[1536,1536]{1,0:T(8,128)(2,1)} %add_convert_fusion.proj_ref, s32[1536,1]{1,0:T(8,128)} %broadcast_in_dim.40.key_ids, s32[1,768]{1,0:T(1,128)} %broadcast_in_dim.17.query_ids, bf16[512,768]{1,0:T(8,128)(2,1)} %get-tuple-element.18.out_ref, ...), custom_call_target="tpu_custom_call" | custom-call | flops 6442450944 | bytes 12582912 | tf_op jit(solution)/shard_map/attend_backward/pallas_call | solution.py:228
  418.9 10.0 %fusion.124 = f32[1536,1024]{1,0:T(8,128)} fusion(bf16[1536,1536]{1,0:T(8,128)(2,1)} %attend_backward.1, bf16[1536,1024]{1,0:T(8,128)(2,1)} %slice_dynamic-update-slice_fusion), kind=kOutput, calls=%fused_computation.400 | convolution fusion | flops 4831838208 | bytes 14155776 | tf_op jit(solution)/shard_map/dot_general | solution.py:28
  433.2 7.7 %fusion.121 = (bf16[1536,1024]{1,0:T(8,128)(2,1)}, f32[1536,1024]{1,0:T(8,128)}) fusion(bf16[1536,1536]{1,0:T(8,128)(2,1)S(1)} %copy-done.13, f32[768,1024]{1,0:T(8,128)S(1)} %fusion.11, f32[768,1024]{1,0:T(8,128)S(1)} %copy-done.17, f32[1024]{0:T(1024)S(1)} %bitcast.126, f32[1024]{0:T(1024)S(1)} %bitcast.128), kind=kOutput, calls=%fused_computation.397 | convolution fusion | flops 4839702528 | bytes 20455424 | tf_op jit(solution)/shard_map/dot_general | solution.py:20
  443.4 3.2 fusion.107
  450.4 12.7 %collective-permute-start.58 = (bf16[144,1024]{1,0:T(8,128)(2,1)S(1)}, bf16[144,1024]{1,0:T(8,128)(2,1)S(1)}, u32[]{:S(2)}, u32[]{:S(2)}) collective-permute-start(bf16[144,1024]{1,0:T(8,128)(2,1)S(1)} %pad_maximum_fusion.13), channel_id=1, source_target_pairs={{0,2},{2,4},{4,6},{6,7},{7,5},{5,3},{3,1},{1,0},{8,10},{10,12},{12... | collective-permute-start | bytes 884744 | tf_op jit(solution)/shard_map/ppermute | solution.py:47
  468.1 7.5 %collective-permute-done.98 = bf16[128,1024]{1,0:T(8,128)(2,1)S(1)} collective-permute-done((bf16[128,1024]{1,0:T(8,128)(2,1)S(1)}, bf16[128,1024]{1,0:T(8,128)(2,1)S(1)}, u32[]{:S(2)}, u32[]{:S(2)}) %collective-permute-start.98) | collective-permute-done | bytes 262176 | tf_op jit(solution)/shard_map/ppermute | solution.py:47
  481.8 10.2 %collective-permute-done.66 = bf16[144,1024]{1,0:T(8,128)(2,1)S(1)} collective-permute-done((bf16[144,1024]{1,0:T(8,128)(2,1)S(1)}, bf16[144,1024]{1,0:T(8,128)(2,1)S(1)}, u32[]{:S(2)}, u32[]{:S(2)}) %collective-permute-start.66) | collective-permute-done | bytes 294944 | tf_op jit(solution)/shard_map/ppermute | solution.py:47
  495.9 5.6 collective-permute-done.67
  504.0 6.3 collective-permute-done.68
  512.7 5.4 collective-permute-done.69
  521.1 4.1 collective-permute-done.70
  528.7 3.4 collective-permute-done.71
  533.4 2.9 slice_add_fusion
  549.2 9.8 %collective-permute-done.56 = bf16[768,512]{1,0:T(8,128)(2,1)} collective-permute-done((bf16[768,512]{1,0:T(8,128)(2,1)}, bf16[768,512]{1,0:T(8,128)(2,1)}, u32[]{:S(2)}, u32[]{:S(2)}) %collective-permute-start.56) | collective-permute-done | bytes 786464 | tf_op jit(solution)/shard_map/ppermute | solution.py:460
  561.1 73.4 %psum.7 = f32[6,512]{1,0:T(8,128)S(1)} all-reduce(f32[6,512]{1,0:T(8,128)S(1)} %stack.71), channel_id=1, replica_groups=mesh['dp'=2,'row'=2,'col'=8] {'dp','col'}, use_global_device_ids=true, to_apply=%region_17.18 | all-reduce | flops 3072 | bytes 24576 | tf_op jit(solution)/shard_map/psum | solution.py:557
  635.2 3.7 slice_add_fusion.2
  (624 shorter events, 272.9 us)
Async XLA Ops:
  2.7 24.3 %collective-permute-start.37 = (bf16[256,512]{1,0:T(8,128)(2,1)}, bf16[256,512]{1,0:T(8,128)(2,1)}, u32[]{:S(2)}, u32[]{:S(2)}) collective-permute-start(bf16[256,512]{1,0:T(8,128)(2,1)} %get-tuple-element.185), channel_id=1, source_target_pairs={{0,8},{8,0},{1,9},{9,1},{2,10},{10,2},{3,11},{11,3},{4,12},{12,4},... | collective-permute-start | bytes 786440 | tf_op jit(solution)/shard_map/ppermute | solution.py:68
  5.2 25.1 %collective-permute-start.22 = (bf16[256,512]{1,0:T(8,128)(2,1)}, bf16[256,512]{1,0:T(8,128)(2,1)}, u32[]{:S(2)}, u32[]{:S(2)}) collective-permute-start(bf16[256,512]{1,0:T(8,128)(2,1)} %get-tuple-element.181), channel_id=1, source_target_pairs={{0,8},{8,0},{1,9},{9,1},{2,10},{10,2},{3,11},{11,3},{4,12},{12,4},... | collective-permute-start | bytes 786440 | tf_op jit(solution)/shard_map/ppermute | solution.py:68
  6.9 14.3 %collective-permute-start.2 = (bf16[192,512]{1,0:T(8,128)(2,1)}, bf16[192,512]{1,0:T(8,128)(2,1)}, u32[]{:S(2)}, u32[]{:S(2)}) collective-permute-start(bf16[192,512]{1,0:T(8,128)(2,1)} %bitcast.6), channel_id=1, source_target_pairs={{0,8},{8,0},{1,9},{9,1},{2,10},{10,2},{3,11},{11,3},{4,12},{12,4},... | collective-permute-start | bytes 589832 | tf_op jit(solution)/shard_map/ppermute | solution.py:68
  30.2 14.0 %collective-permute-start.39 = (bf16[128,1024]{1,0:T(8,128)(2,1)S(1)}, bf16[128,1024]{1,0:T(8,128)(2,1)S(1)}, u32[]{:S(2)}, u32[]{:S(2)}) collective-permute-start(bf16[128,1024]{1,0:T(8,128)(2,1)S(1)} %get-tuple-element.182), channel_id=1, source_target_pairs={{2,0},{4,2},{6,4},{7,6},{5,7},{3,5},{1,3},{0,1},{10,8},{12,10},{14... | collective-permute-start | bytes 786440 | tf_op jit(solution)/shard_map/ppermute | solution.py:47
  31.3 14.4 %collective-permute-start.23 = (bf16[128,1024]{1,0:T(8,128)(2,1)S(1)}, bf16[128,1024]{1,0:T(8,128)(2,1)S(1)}, u32[]{:S(2)}, u32[]{:S(2)}) collective-permute-start(bf16[128,1024]{1,0:T(8,128)(2,1)S(1)} %get-tuple-element.179), channel_id=1, source_target_pairs={{0,2},{2,4},{4,6},{6,7},{7,5},{5,3},{3,1},{1,0},{8,10},{10,12},{12... | collective-permute-start | bytes 786440 | tf_op jit(solution)/shard_map/ppermute | solution.py:47
  34.0 14.1 %collective-permute-start.24 = (bf16[128,1024]{1,0:T(8,128)(2,1)S(1)}, bf16[128,1024]{1,0:T(8,128)(2,1)S(1)}, u32[]{:S(2)}, u32[]{:S(2)}) collective-permute-start(bf16[128,1024]{1,0:T(8,128)(2,1)S(1)} %get-tuple-element.178), channel_id=1, source_target_pairs={{2,0},{4,2},{6,4},{7,6},{5,7},{3,5},{1,3},{0,1},{10,8},{12,10},{14... | collective-permute-start | bytes 786440 | tf_op jit(solution)/shard_map/ppermute | solution.py:47
  37.7 40.8 %collective-permute-start = (bf16[768,512]{1,0:T(8,128)(2,1)S(1)}, bf16[768,512]{1,0:T(8,128)(2,1)S(1)}, u32[]{:S(2)}, u32[]{:S(2)}) collective-permute-start(bf16[768,512]{1,0:T(8,128)(2,1)S(1)} %copy-done.6), channel_id=1, source_target_pairs={{0,8},{8,0},{1,9},{9,1},{2,10},{10,2},{3,11},{11,3},{4,12},{12,4},... | collective-permute-start | bytes 2359304 | tf_op jit(solution)/shard_map/ppermute | solution.py:68
  39.6 40.6 %collective-permute-start.18 = (bf16[768,512]{1,0:T(8,128)(2,1)S(1)}, bf16[768,512]{1,0:T(8,128)(2,1)S(1)}, u32[]{:S(2)}, u32[]{:S(2)}) collective-permute-start(bf16[768,512]{1,0:T(8,128)(2,1)S(1)} %copy-done.6), channel_id=1, source_target_pairs={{0,1},{1,2},{2,3},{4,5},{5,6},{6,7},{8,9},{9,10},{10,11},{12,13},{... | collective-permute-start | bytes 2359304 | tf_op jit(solution)/shard_map/ppermute | solution.py:322
  44.3 23.0 %collective-permute-start.40 = (bf16[128,1024]{1,0:T(8,128)(2,1)S(1)}, bf16[128,1024]{1,0:T(8,128)(2,1)S(1)}, u32[]{:S(2)}, u32[]{:S(2)}) collective-permute-start(bf16[128,1024]{1,0:T(8,128)(2,1)S(1)} %collective-permute-done.39), channel_id=1, source_target_pairs={{2,0},{4,2},{6,4},{7,6},{5,7},{3,5},{1,3},{0,1},{10,8},{12,10},{14... | collective-permute-start | bytes 786440 | tf_op jit(solution)/shard_map/ppermute | solution.py:47
  45.7 24.0 %collective-permute-start.46 = (bf16[128,1024]{1,0:T(8,128)(2,1)S(1)}, bf16[128,1024]{1,0:T(8,128)(2,1)S(1)}, u32[]{:S(2)}, u32[]{:S(2)}) collective-permute-start(bf16[128,1024]{1,0:T(8,128)(2,1)S(1)} %collective-permute-done.38), channel_id=1, source_target_pairs={{0,2},{2,4},{4,6},{6,7},{7,5},{5,3},{3,1},{1,0},{8,10},{10,12},{12... | collective-permute-start | bytes 786440 | tf_op jit(solution)/shard_map/ppermute | solution.py:47
  48.1 33.0 %collective-permute-start.53 = (bf16[768,512]{1,0:T(8,128)(2,1)S(1)}, bf16[768,512]{1,0:T(8,128)(2,1)S(1)}, u32[]{:S(2)}, u32[]{:S(2)}) collective-permute-start(bf16[768,512]{1,0:T(8,128)(2,1)S(1)} %copy-done.18), channel_id=1, source_target_pairs={{0,8},{8,0},{1,9},{9,1},{2,10},{10,2},{3,11},{11,3},{4,12},{12,4},... | collective-permute-start | bytes 2359304 | tf_op jit(solution)/shard_map/ppermute | solution.py:68
  74.7 14.7 %collective-permute-start.12 = (bf16[144,1024]{1,0:T(8,128)(2,1)S(1)}, bf16[144,1024]{1,0:T(8,128)(2,1)S(1)}, u32[]{:S(2)}, u32[]{:S(2)}) collective-permute-start(bf16[144,1024]{1,0:T(8,128)(2,1)S(1)} %collective-permute-done.4), channel_id=1, source_target_pairs={{0,2},{2,4},{4,6},{6,7},{7,5},{5,3},{3,1},{1,0},{8,10},{10,12},{12... | collective-permute-start | bytes 884744 | tf_op jit(solution)/shard_map/ppermute | solution.py:47
  78.5 14.5 %collective-permute-start.41 = (bf16[128,1024]{1,0:T(8,128)(2,1)S(1)}, bf16[128,1024]{1,0:T(8,128)(2,1)S(1)}, u32[]{:S(2)}, u32[]{:S(2)}) collective-permute-start(bf16[128,1024]{1,0:T(8,128)(2,1)S(1)} %collective-permute-done.40), channel_id=1, source_target_pairs={{2,0},{4,2},{6,4},{7,6},{5,7},{3,5},{1,3},{0,1},{10,8},{12,10},{14... | collective-permute-start | bytes 786440 | tf_op jit(solution)/shard_map/ppermute | solution.py:47
  80.3 14.8 %collective-permute-start.47 = (bf16[128,1024]{1,0:T(8,128)(2,1)S(1)}, bf16[128,1024]{1,0:T(8,128)(2,1)S(1)}, u32[]{:S(2)}, u32[]{:S(2)}) collective-permute-start(bf16[128,1024]{1,0:T(8,128)(2,1)S(1)} %collective-permute-done.46), channel_id=1, source_target_pairs={{0,2},{2,4},{4,6},{6,7},{7,5},{5,3},{3,1},{1,0},{8,10},{10,12},{12... | collective-permute-start | bytes 786440 | tf_op jit(solution)/shard_map/ppermute | solution.py:47
  81.1 17.5 %collective-permute-start.26 = (bf16[128,1024]{1,0:T(8,128)(2,1)S(1)}, bf16[128,1024]{1,0:T(8,128)(2,1)S(1)}, u32[]{:S(2)}, u32[]{:S(2)}) collective-permute-start(bf16[128,1024]{1,0:T(8,128)(2,1)S(1)} %collective-permute-done.25), channel_id=1, source_target_pairs={{2,0},{4,2},{6,4},{7,6},{5,7},{3,5},{1,3},{0,1},{10,8},{12,10},{14... | collective-permute-start | bytes 786440 | tf_op jit(solution)/shard_map/ppermute | solution.py:47
  89.4 15.5 %collective-permute-start.7 = (bf16[144,1024]{1,0:T(8,128)(2,1)S(1)}, bf16[144,1024]{1,0:T(8,128)(2,1)S(1)}, u32[]{:S(2)}, u32[]{:S(2)}) collective-permute-start(bf16[144,1024]{1,0:T(8,128)(2,1)S(1)} %collective-permute-done.6), channel_id=1, source_target_pairs={{2,0},{4,2},{6,4},{7,6},{5,7},{3,5},{1,3},{0,1},{10,8},{12,10},{14... | collective-permute-start | bytes 884744 | tf_op jit(solution)/shard_map/ppermute | solution.py:47
  95.0 15.5 %collective-permute-start.42 = (bf16[128,1024]{1,0:T(8,128)(2,1)S(1)}, bf16[128,1024]{1,0:T(8,128)(2,1)S(1)}, u32[]{:S(2)}, u32[]{:S(2)}) collective-permute-start(bf16[128,1024]{1,0:T(8,128)(2,1)S(1)} %collective-permute-done.41), channel_id=1, source_target_pairs={{2,0},{4,2},{6,4},{7,6},{5,7},{3,5},{1,3},{0,1},{10,8},{12,10},{14... | collective-permute-start | bytes 786440 | tf_op jit(solution)/shard_map/ppermute | solution.py:47
  98.6 36.1 %collective-permute-start.19 = (bf16[768,512]{1,0:T(8,128)(2,1)S(1)}, bf16[768,512]{1,0:T(8,128)(2,1)S(1)}, u32[]{:S(2)}, u32[]{:S(2)}) collective-permute-start(bf16[768,512]{1,0:T(8,128)(2,1)S(1)} %collective-permute-done.18), channel_id=1, source_target_pairs={{0,8},{8,0},{1,9},{9,1},{2,10},{10,2},{3,11},{11,3},{4,12},{12,4},... | collective-permute-start | bytes 2359304 | tf_op jit(solution)/shard_map/ppermute | solution.py:68
  129.1 13.0 %collective-permute-start.15 = (bf16[144,1024]{1,0:T(8,128)(2,1)S(1)}, bf16[144,1024]{1,0:T(8,128)(2,1)S(1)}, u32[]{:S(2)}, u32[]{:S(2)}) collective-permute-start(bf16[144,1024]{1,0:T(8,128)(2,1)S(1)} %collective-permute-done.14), channel_id=1, source_target_pairs={{0,2},{2,4},{4,6},{6,7},{7,5},{5,3},{3,1},{1,0},{8,10},{10,12},{12... | collective-permute-start | bytes 884744 | tf_op jit(solution)/shard_map/ppermute | solution.py:47
  134.7 13.0 %collective-permute-start.50 = (bf16[128,1024]{1,0:T(8,128)(2,1)S(1)}, bf16[128,1024]{1,0:T(8,128)(2,1)S(1)}, u32[]{:S(2)}, u32[]{:S(2)}) collective-permute-start(bf16[128,1024]{1,0:T(8,128)(2,1)S(1)} %collective-permute-done.49), channel_id=1, source_target_pairs={{0,2},{2,4},{4,6},{6,7},{7,5},{5,3},{3,1},{1,0},{8,10},{10,12},{12... | collective-permute-start | bytes 786440 | tf_op jit(solution)/shard_map/ppermute | solution.py:47
  136.4 14.9 %collective-permute-start.29 = (bf16[128,1024]{1,0:T(8,128)(2,1)S(1)}, bf16[128,1024]{1,0:T(8,128)(2,1)S(1)}, u32[]{:S(2)}, u32[]{:S(2)}) collective-permute-start(bf16[128,1024]{1,0:T(8,128)(2,1)S(1)} %collective-permute-done.28), channel_id=1, source_target_pairs={{2,0},{4,2},{6,4},{7,6},{5,7},{3,5},{1,3},{0,1},{10,8},{12,10},{14... | collective-permute-start | bytes 786440 | tf_op jit(solution)/shard_map/ppermute | solution.py:47
  140.1 13.3 %collective-permute-start.35 = (bf16[128,1024]{1,0:T(8,128)(2,1)S(1)}, bf16[128,1024]{1,0:T(8,128)(2,1)}, u32[]{:S(2)}, u32[]{:S(2)}) collective-permute-start(bf16[128,1024]{1,0:T(8,128)(2,1)S(1)} %collective-permute-done.34), channel_id=1, source_target_pairs={{0,2},{2,4},{4,6},{6,7},{7,5},{5,3},{3,1},{1,0},{8,10},{10,12},{12... | collective-permute-start | bytes 786440 | tf_op jit(solution)/shard_map/ppermute | solution.py:47
  142.1 15.5 %collective-permute-start.10 = (bf16[144,1024]{1,0:T(8,128)(2,1)S(1)}, bf16[144,1024]{1,0:T(8,128)(2,1)S(1)}, u32[]{:S(2)}, u32[]{:S(2)}) collective-permute-start(bf16[144,1024]{1,0:T(8,128)(2,1)S(1)} %collective-permute-done.9), channel_id=1, source_target_pairs={{2,0},{4,2},{6,4},{7,6},{5,7},{3,5},{1,3},{0,1},{10,8},{12,10},{14... | collective-permute-start | bytes 884744 | tf_op jit(solution)/shard_map/ppermute | solution.py:47
  145.7 14.0 %collective-permute-start.16 = (bf16[144,1024]{1,0:T(8,128)(2,1)S(1)}, bf16[144,1024]{1,0:T(8,128)(2,1)S(1)}, u32[]{:S(2)}, u32[]{:S(2)}) collective-permute-start(bf16[144,1024]{1,0:T(8,128)(2,1)S(1)} %collective-permute-done.15), channel_id=1, source_target_pairs={{0,2},{2,4},{4,6},{6,7},{7,5},{5,3},{3,1},{1,0},{8,10},{10,12},{12... | collective-permute-start | bytes 884744 | tf_op jit(solution)/shard_map/ppermute | solution.py:47
  147.7 15.5 %collective-permute-start.45 = (bf16[128,1024]{1,0:T(8,128)(2,1)S(1)}, bf16[128,1024]{1,0:T(8,128)(2,1)S(1)}, u32[]{:S(2)}, u32[]{:S(2)}) collective-permute-start(bf16[128,1024]{1,0:T(8,128)(2,1)S(1)} %collective-permute-done.44), channel_id=1, source_target_pairs={{2,0},{4,2},{6,4},{7,6},{5,7},{3,5},{1,3},{0,1},{10,8},{12,10},{14... | collective-permute-start | bytes 786440 | tf_op jit(solution)/shard_map/ppermute | solution.py:47
  151.3 14.4 %collective-permute-start.51 = (bf16[128,1024]{1,0:T(8,128)(2,1)S(1)}, bf16[128,1024]{1,0:T(8,128)(2,1)S(1)}, u32[]{:S(2)}, u32[]{:S(2)}) collective-permute-start(bf16[128,1024]{1,0:T(8,128)(2,1)S(1)} %collective-permute-done.50), channel_id=1, source_target_pairs={{0,2},{2,4},{4,6},{6,7},{7,5},{5,3},{3,1},{1,0},{8,10},{10,12},{12... | collective-permute-start | bytes 786440 | tf_op jit(solution)/shard_map/ppermute | solution.py:47
  153.3 15.5 %collective-permute-start.30 = (bf16[128,1024]{1,0:T(8,128)(2,1)S(1)}, bf16[128,1024]{1,0:T(8,128)(2,1)S(1)}, u32[]{:S(2)}, u32[]{:S(2)}) collective-permute-start(bf16[128,1024]{1,0:T(8,128)(2,1)S(1)} %collective-permute-done.29), channel_id=1, source_target_pairs={{2,0},{4,2},{6,4},{7,6},{5,7},{3,5},{1,3},{0,1},{10,8},{12,10},{14... | collective-permute-start | bytes 786440 | tf_op jit(solution)/shard_map/ppermute | solution.py:47
  157.6 98.4 %collective-permute-start.36 = (bf16[128,1024]{1,0:T(8,128)(2,1)}, bf16[128,1024]{1,0:T(8,128)(2,1)}, u32[]{:S(2)}, u32[]{:S(2)}) collective-permute-start(bf16[128,1024]{1,0:T(8,128)(2,1)} %collective-permute-done.35), channel_id=1, source_target_pairs={{0,2},{2,4},{4,6},{6,7},{7,5},{5,3},{3,1},{1,0},{8,10},{10,12},{12... | collective-permute-start | bytes 786440 | tf_op jit(solution)/shard_map/ppermute | solution.py:47
  159.6 12.9 %collective-permute-start.11 = (bf16[144,1024]{1,0:T(8,128)(2,1)S(1)}, bf16[144,1024]{1,0:T(8,128)(2,1)S(1)}, u32[]{:S(2)}, u32[]{:S(2)}) collective-permute-start(bf16[144,1024]{1,0:T(8,128)(2,1)S(1)} %collective-permute-done.10), channel_id=1, source_target_pairs={{2,0},{4,2},{6,4},{7,6},{5,7},{3,5},{1,3},{0,1},{10,8},{12,10},{14... | collective-permute-start | bytes 884744 | tf_op jit(solution)/shard_map/ppermute | solution.py:47
  163.2 16.2 %collective-permute-start.17 = (bf16[144,1024]{1,0:T(8,128)(2,1)S(1)}, bf16[144,1024]{1,0:T(8,128)(2,1)S(1)}, u32[]{:S(2)}, u32[]{:S(2)}) collective-permute-start(bf16[144,1024]{1,0:T(8,128)(2,1)S(1)} %collective-permute-done.16), channel_id=1, source_target_pairs={{0,2},{2,4},{4,6},{6,7},{7,5},{5,3},{3,1},{1,0},{8,10},{10,12},{12... | collective-permute-start | bytes 884744 | tf_op jit(solution)/shard_map/ppermute | solution.py:47
  306.7 44.4 %collective-permute-start.52 = (bf16[768,512]{1,0:T(8,128)(2,1)S(1)}, bf16[768,512]{1,0:T(8,128)(2,1)S(1)}, u32[]{:S(2)}, u32[]{:S(2)}) collective-permute-start(bf16[768,512]{1,0:T(8,128)(2,1)S(1)} %slice.1394), channel_id=1, source_target_pairs={{0,8},{8,0},{1,9},{9,1},{2,10},{10,2},{3,11},{11,3},{4,12},{12,4},... | collective-permute-start | bytes 2359304 | tf_op jit(solution)/shard_map/ppermute | solution.py:68
  310.0 20.5 %collective-permute-start.76 = (bf16[128,1024]{1,0:T(8,128)(2,1)S(1)}, bf16[128,1024]{1,0:T(8,128)(2,1)S(1)}, u32[]{:S(2)}, u32[]{:S(2)}) collective-permute-start(bf16[128,1024]{1,0:T(8,128)(2,1)S(1)} %get-tuple-element.146), channel_id=1, source_target_pairs={{0,2},{2,4},{4,6},{6,7},{7,5},{5,3},{3,1},{1,0},{8,10},{10,12},{12... | collective-permute-start | bytes 786440 | tf_op jit(solution)/shard_map/ppermute | solution.py:47
  324.1 64.0 %collective-permute-start.54 = (bf16[768,1024]{1,0:T(8,128)(2,1)S(1)}, bf16[768,1024]{1,0:T(8,128)(2,1)S(1)}, u32[]{:S(2)}, u32[]{:S(2)}) collective-permute-start(bf16[768,1024]{1,0:T(8,128)(2,1)S(1)} %pad_maximum_fusion.3), channel_id=1, source_target_pairs={{0,8},{8,0},{1,9},{9,1},{2,10},{10,2},{3,11},{11,3},{4,12},{12,4},... | collective-permute-start | bytes 4718600 | tf_op jit(solution)/shard_map/ppermute | solution.py:68
  380.4 84.2 %collective-permute-start.81 = (bf16[128,1024]{1,0:T(8,128)(2,1)}, bf16[128,1024]{1,0:T(8,128)(2,1)S(1)}, u32[]{:S(2)}, u32[]{:S(2)}) collective-permute-start(bf16[128,1024]{1,0:T(8,128)(2,1)} %get-tuple-element.120), channel_id=1, source_target_pairs={{0,2},{2,4},{4,6},{6,7},{7,5},{5,3},{3,1},{1,0},{8,10},{10,12},{12... | collective-permute-start | bytes 786440 | tf_op jit(solution)/shard_map/ppermute | solution.py:47
  382.5 84.2 %collective-permute-start.88 = (bf16[128,1024]{1,0:T(8,128)(2,1)}, bf16[128,1024]{1,0:T(8,128)(2,1)}, u32[]{:S(2)}, u32[]{:S(2)}) collective-permute-start(bf16[128,1024]{1,0:T(8,128)(2,1)} %get-tuple-element.121), channel_id=1, source_target_pairs={{2,0},{4,2},{6,4},{7,6},{5,7},{3,5},{1,3},{0,1},{10,8},{12,10},{14... | collective-permute-start | bytes 786440 | tf_op jit(solution)/shard_map/ppermute | solution.py:47
  386.1 62.9 %collective-permute-start.97 = (bf16[128,1024]{1,0:T(8,128)(2,1)}, bf16[128,1024]{1,0:T(8,128)(2,1)}, u32[]{:S(2)}, u32[]{:S(2)}) collective-permute-start(bf16[128,1024]{1,0:T(8,128)(2,1)} %get-tuple-element.106), channel_id=1, source_target_pairs={{0,2},{2,4},{4,6},{6,7},{7,5},{5,3},{3,1},{1,0},{8,10},{10,12},{12... | collective-permute-start | bytes 786440 | tf_op jit(solution)/shard_map/ppermute | solution.py:47
  388.1 62.3 %collective-permute-start.104 = (bf16[128,1024]{1,0:T(8,128)(2,1)}, bf16[128,1024]{1,0:T(8,128)(2,1)}, u32[]{:S(2)}, u32[]{:S(2)}) collective-permute-start(bf16[128,1024]{1,0:T(8,128)(2,1)} %get-tuple-element.107), channel_id=1, source_target_pairs={{2,0},{4,2},{6,4},{7,6},{5,7},{3,5},{1,3},{0,1},{10,8},{12,10},{14... | collective-permute-start | bytes 786440 | tf_op jit(solution)/shard_map/ppermute | solution.py:47
  443.4 90.0 %collective-permute-start.55 = (bf16[1536,512]{1,0:T(8,128)(2,1)S(1)}, bf16[1536,512]{1,0:T(8,128)(2,1)}, u32[]{:S(2)}, u32[]{:S(2)}) collective-permute-start(bf16[1536,512]{1,0:T(8,128)(2,1)S(1)} %slice.1392), channel_id=1, source_target_pairs={{0,8},{8,0},{1,9},{9,1},{2,10},{10,2},{3,11},{11,3},{4,12},{12,4},... | collective-permute-start | bytes 4718600 | tf_op jit(solution)/shard_map/ppermute | solution.py:68
  449.0 30.5 %collective-permute-start.65 = (bf16[144,1024]{1,0:T(8,128)(2,1)S(1)}, bf16[144,1024]{1,0:T(8,128)(2,1)S(1)}, u32[]{:S(2)}, u32[]{:S(2)}) collective-permute-start(bf16[144,1024]{1,0:T(8,128)(2,1)S(1)} %pad_maximum_fusion.14), channel_id=1, source_target_pairs={{2,0},{4,2},{6,4},{7,6},{5,7},{3,5},{1,3},{0,1},{10,8},{12,10},{14... | collective-permute-start | bytes 884744 | tf_op jit(solution)/shard_map/ppermute | solution.py:47
  450.4 29.3 %collective-permute-start.58 = (bf16[144,1024]{1,0:T(8,128)(2,1)S(1)}, bf16[144,1024]{1,0:T(8,128)(2,1)S(1)}, u32[]{:S(2)}, u32[]{:S(2)}) collective-permute-start(bf16[144,1024]{1,0:T(8,128)(2,1)S(1)} %pad_maximum_fusion.13), channel_id=1, source_target_pairs={{0,2},{2,4},{4,6},{6,7},{7,5},{5,3},{3,1},{1,0},{8,10},{10,12},{12... | collective-permute-start | bytes 884744 | tf_op jit(solution)/shard_map/ppermute | solution.py:47
  475.6 16.9 %collective-permute-start.82 = (bf16[128,1024]{1,0:T(8,128)(2,1)S(1)}, bf16[128,1024]{1,0:T(8,128)(2,1)S(1)}, u32[]{:S(2)}, u32[]{:S(2)}) collective-permute-start(bf16[128,1024]{1,0:T(8,128)(2,1)S(1)} %get-tuple-element.118), channel_id=1, source_target_pairs={{0,2},{2,4},{4,6},{6,7},{7,5},{5,3},{3,1},{1,0},{8,10},{10,12},{12... | collective-permute-start | bytes 786440 | tf_op jit(solution)/shard_map/ppermute | solution.py:47
  478.1 16.5 %collective-permute-start.89 = (bf16[128,1024]{1,0:T(8,128)(2,1)S(1)}, bf16[128,1024]{1,0:T(8,128)(2,1)S(1)}, u32[]{:S(2)}, u32[]{:S(2)}) collective-permute-start(bf16[128,1024]{1,0:T(8,128)(2,1)S(1)} %get-tuple-element.119), channel_id=1, source_target_pairs={{2,0},{4,2},{6,4},{7,6},{5,7},{3,5},{1,3},{0,1},{10,8},{12,10},{14... | collective-permute-start | bytes 786440 | tf_op jit(solution)/shard_map/ppermute | solution.py:47
  512.6 15.0 %collective-permute-start.107 = (bf16[512,512]{1,0:T(8,128)(2,1)S(1)}, bf16[512,512]{1,0:T(8,128)(2,1)S(1)}, u32[]{:S(2)}, u32[]{:S(2)}) collective-permute-start(bf16[512,512]{1,0:T(8,128)(2,1)S(1)} %pad_maximum_fusion.9), channel_id=1, source_target_pairs={{0,16},{16,0},{1,17},{17,1},{2,18},{18,2},{3,19},{19,3},{4,20},{20... | collective-permute-start | bytes 1572872 | tf_op jit(solution)/shard_map/ppermute | solution.py:310
  521.1 22.8 %collective-permute-start.90 = (bf16[256,512]{1,0:T(8,128)(2,1)}, bf16[256,512]{1,0:T(8,128)(2,1)}, u32[]{:S(2)}, u32[]{:S(2)}) collective-permute-start(bf16[256,512]{1,0:T(8,128)(2,1)} %pad_maximum_fusion.16), channel_id=1, source_target_pairs={{0,8},{8,0},{1,9},{9,1},{2,10},{10,2},{3,11},{11,3},{4,12},{12,4},... | collective-permute-start | bytes 786440 | tf_op jit(solution)/shard_map/ppermute | solution.py:68
  537.3 21.8 %collective-permute-start.56 = (bf16[768,512]{1,0:T(8,128)(2,1)}, bf16[768,512]{1,0:T(8,128)(2,1)}, u32[]{:S(2)}, u32[]{:S(2)}) collective-permute-start(bf16[768,512]{1,0:T(8,128)(2,1)} %slice.1393), channel_id=1, source_target_pairs={{1,0},{2,1},{3,2},{5,4},{6,5},{7,6},{9,8},{10,9},{11,10},{13,12},{... | collective-permute-start | bytes 2359304 | tf_op jit(solution)/shard_map/ppermute | solution.py:460
  546.3 92.6 %collective-permute-start.73 = (bf16[512,512]{1,0:T(8,128)(2,1)}, bf16[512,512]{1,0:T(8,128)(2,1)}, u32[]{:S(2)}, u32[]{:S(2)}) collective-permute-start(bf16[512,512]{1,0:T(8,128)(2,1)} %pad_maximum_fusion.7), channel_id=1, source_target_pairs={{0,16},{16,0},{1,17},{17,1},{2,18},{18,2},{3,19},{19,3},{4,20},{20... | collective-permute-start | bytes 1572872 | tf_op jit(solution)/shard_map/ppermute | solution.py:310
  547.6 94.6 %collective-permute-start.91 = (bf16[512,512]{1,0:T(8,128)(2,1)}, bf16[512,512]{1,0:T(8,128)(2,1)}, u32[]{:S(2)}, u32[]{:S(2)}) collective-permute-start(bf16[512,512]{1,0:T(8,128)(2,1)} %pad_maximum_fusion.8), channel_id=1, source_target_pairs={{0,16},{16,0},{1,17},{17,1},{2,18},{18,2},{3,19},{19,3},{4,20},{20... | collective-permute-start | bytes 1572872 | tf_op jit(solution)/shard_map/ppermute | solution.py:310
  561.0 74.2 %collective-permute-start.57 = (f32[768,2]{0,1:T(2,128)S(1)}, f32[768,2]{0,1:T(2,128)S(1)}, u32[]{:S(2)}, u32[]{:S(2)}) collective-permute-start(f32[768,2]{0,1:T(2,128)S(1)} %pad_maximum_fusion.19), channel_id=1, source_target_pairs={{0,8},{8,0},{1,9},{9,1},{2,10},{10,2},{3,11},{11,3},{4,12},{12,4},... | collective-permute-start | bytes 18440 | tf_op jit(solution)/shard_map/ppermute | solution.py:68
  (159 other events, 2780.8 us)

commit v2 on v1

v2 whole, which is shorter than its diff:
```python
import math
from functools import partial

import jax
import jax.numpy as jnp
from jax import lax
from jax.experimental import pallas as pl
from jax.experimental.pallas import tpu as pltpu
from jax.sharding import PartitionSpec as P

HD = 64

epsilon = 1e-05
masked_score = -1000000000.0
low = jnp.bfloat16
full = jnp.float32


def dot_nn(left, right):
    return lax.dot_general(left, right, (((1,), (0,)), ((), ())), preferred_element_type=full)


def dot_nt(left, right):
    return lax.dot_general(left, right, (((1,), (1,)), ((), ())), preferred_element_type=full)


def dot_tn(left, right):
    return lax.dot_general(left, right, (((0,), (0,)), ((), ())), preferred_element_type=full)


def ring_order(count):
    across = {8: 2, 16: 4}.get(count, 1)
    along = count // across
    order = [z * across for z in range(along)]
    for step in range(along):
        z = along - 1 - step
        turn = range(1, across) if step % 2 == 0 else range(across - 1, 0, -1)
        order += [z * across + y for y in turn]
    return order


def shift(values, count, backward):
    order = ring_order(count)
    pairs = [(order[i], order[(i + 1) % count]) for i in range(count)]
    if backward:
        pairs = [(b, a) for a, b in pairs]
    return lax.ppermute(values, "col", pairs)


def distances(count):
    return sorted(range(count), key=lambda t: (min(t, count - t), t))


def after(values, *others):
    return lax.optimization_barrier((values, *others))[0]


def ring_gather(block, count):
    mid = block.shape[0] // 2
    reach = count // 2
    pieces = {0: [(block, 0)]}
    ahead = behind = block
    for t in range(1, reach):
        ahead, behind = shift(ahead, count, False), shift(behind, count, True)
        pieces[t], pieces[count - t] = [(ahead, 0)], [(behind, 0)]
    ahead, behind = shift(ahead[:mid], count, False), shift(behind[mid:], count, True)
    pieces[reach] = [(ahead, 0), (behind, mid)]
    return pieces


def ring_scatter(blocks, count):
    reach = count // 2
    mid = blocks[0].shape[0] // 2

    def add(block, other):
        return (block.astype(full) + other.astype(full)).astype(low)

    ahead = shift(blocks[reach][:mid].astype(low), count, False)
    behind = shift(blocks[reach][mid:].astype(low), count, True)
    for t in range(reach - 1, 0, -1):
        one, two = blocks[count - t], blocks[t]
        if t == reach - 1:
            one = jnp.concatenate([add(one[:mid], ahead), one[mid:].astype(low)])
            two = jnp.concatenate([two[:mid].astype(low), add(two[mid:], behind)])
        else:
            one, two = add(one, ahead), add(two, behind)
        ahead, behind = shift(one, count, False), shift(two, count, True)
    if reach == 1:
        ahead = jnp.concatenate([ahead, jnp.zeros_like(behind)])
        behind = jnp.concatenate([jnp.zeros_like(ahead[:mid]), behind])
    return blocks[0].astype(full) + ahead.astype(full) + behind.astype(full)


def join(pieces, order, rows):
    sources, places = [], {}
    copies = []
    for number, (first, past) in enumerate(rows):
        for at, t in enumerate(order):
            for block, base in pieces[t]:
                if id(block) not in places:
                    places[id(block)] = len(sources)
                    sources.append(block)
                low_row, high_row = max(first, base), min(past, base + block.shape[0])
                if low_row < high_row:
                    copies.append(
                        (
                            places[id(block)],
                            low_row - base,
                            number,
                            at * (past - first) + low_row - first,
                            high_row - low_row,
                        )
                    )
    width = sources[0].shape[1]

    def kernel(*refs):
        for source, start, number, to, size in copies:
            refs[len(sources) + number][to : to + size, :] = refs[source][start : start + size, :]

    shapes = [
        jax.ShapeDtypeStruct((len(order) * (past - first), width), low) for first, past in rows
    ]
    moved = sum(math.prod(v.shape) for v in shapes) * 4
    return pl.pallas_call(
        kernel,
        out_shape=shapes,
        in_specs=[pl.BlockSpec(memory_space=pltpu.VMEM)] * len(sources),
        out_specs=[pl.BlockSpec(memory_space=pltpu.VMEM)] * len(shapes),
        cost_estimate=pl.CostEstimate(flops=0, bytes_accessed=moved, transcendentals=0),
        name="join",
    )(*sources)


def sum_over(values, axis):
    count = lax.axis_size(axis)
    if count & (count - 1):
        return lax.psum(values, axis)
    step = 1
    while step < count:
        values = values + lax.ppermute(values, axis, [(c, c ^ step) for c in range(count)])
        step *= 2
    return values


def swap(values):
    return lax.ppermute(values, "row", [(0, 1), (1, 0)])


def masks_of(blk, own, key_ids, query_ids, i):
    ids = query_ids[:, i * blk : (i + 1) * blk]

    def mask(at, diagonal):
        same = key_ids[pl.ds(at, blk), :] == ids
        if diagonal:
            rows = lax.broadcasted_iota(jnp.int32, (blk, blk), 0)
            columns = lax.broadcasted_iota(jnp.int32, (blk, blk), 1)
            same = same & (rows <= columns)
        return same

    return mask


def forward_kernel(blk, own, group, low_ref, proj_ref, key_ids, query_ids, out_ref, lse_ref, keys):
    for g in range(group):
        keys[g] = jnp.transpose(proj_ref[(3 * g + 1) * HD : (3 * g + 2) * HD, :])

    for i in range(query_ids.shape[1] // blk):
        mask = masks_of(blk, own, key_ids, query_ids, i)
        start = own + i * blk
        queries = [
            proj_ref[3 * g * HD : (3 * g + 1) * HD, start : start + blk]
            * jnp.asarray(HD**-0.5, low)
            for g in range(group)
        ]

        def values(g, at):
            return proj_ref[(3 * g + 2) * HD : (3 * g + 3) * HD, pl.ds(at, blk)]

        allowed = mask(start, True)
        carry = []
        for g in range(group):
            scores = dot_nn(keys[g, pl.ds(start, blk), :], queries[g])
            scores = jnp.where(allowed, scores, masked_score)
            highest = jnp.max(scores, axis=0, keepdims=True)
            weights = jnp.exp(scores - highest)
            total = jnp.sum(weights, axis=0, keepdims=True)
            carry.append((highest, total, dot_nn(values(g, start), weights.astype(low))))

        def body(j, carry):
            at = pl.multiple_of(j * blk, blk)
            allowed = mask(at, False)
            later = []
            for g, (before, total, acc) in enumerate(carry):
                scores = dot_nn(keys[g, pl.ds(at, blk), :], queries[g])
                scores = jnp.where(allowed, scores, masked_score)
                highest = jnp.maximum(before, jnp.max(scores, axis=0, keepdims=True))
                shrink = jnp.exp(before - highest)
                weights = jnp.exp(scores - highest)
                total = total * shrink + jnp.sum(weights, axis=0, keepdims=True)
                acc = acc * shrink + dot_nn(values(g, at), weights.astype(low))
                later.append((highest, total, acc))
            return tuple(later)

        carry = lax.fori_loop(low_ref[i], own // blk + i, body, tuple(carry))
        for g, (highest, total, acc) in enumerate(carry):
            here = slice(i * blk, (i + 1) * blk)
            out_ref[g * HD : (g + 1) * HD, here] = (acc / total).astype(low)
            lse_ref[g * 8 : g * 8 + 1, here] = highest + jnp.log(total)


def backward_kernel(
    blk,
    own,
    group,
    low_ref,
    proj_ref,
    key_ids,
    query_ids,
    out_ref,
    lse_ref,
    grad_ref,
    grad_proj,
    keys,
    values,
    grad_keys,
    grad_values,
):
    for g in range(group):
        keys[g] = jnp.transpose(proj_ref[(3 * g + 1) * HD : (3 * g + 2) * HD, :])
        values[g] = jnp.transpose(proj_ref[(3 * g + 2) * HD : (3 * g + 3) * HD, :])
        grad_proj[3 * g * HD : (3 * g + 1) * HD, 0:own] = jnp.zeros((HD, own), low)
    grad_keys[...] = jnp.zeros_like(grad_keys)
    grad_values[...] = jnp.zeros_like(grad_values)

    for i in range(query_ids.shape[1] // blk):
        mask = masks_of(blk, own, key_ids, query_ids, i)
        start = own + i * blk
        here = slice(i * blk, (i + 1) * blk)
        queries, against, grads, summary = [], [], [], []
        for g in range(group):
            head = slice(g * HD, (g + 1) * HD)
            queries.append(
                proj_ref[3 * g * HD : (3 * g + 1) * HD, start : start + blk]
                * jnp.asarray(HD**-0.5, low)
            )
            grads.append(grad_ref[head, here])
            product = out_ref[head, here].astype(full) * grads[g].astype(full)
            against.append(jnp.sum(product, axis=0, keepdims=True))
            summary.append(lse_ref[g * 8 : g * 8 + 1, here])

        def blocks(at, diagonal):
            allowed = mask(at, diagonal)
            found = []
            for g in range(group):
                scores = dot_nn(keys[g, pl.ds(at, blk), :], queries[g])
                chances = jnp.exp(jnp.where(allowed, scores, masked_score) - summary[g])
                grad_chances = dot_nn(values[g, pl.ds(at, blk), :], grads[g])
                grad_values[g, :, pl.ds(at, blk)] += dot_nt(grads[g], chances.astype(low))
                grad_scores = (chances * (grad_chances - against[g])).astype(low)
                grad_keys[g, :, pl.ds(at, blk)] += dot_nt(queries[g], grad_scores)
                rows = proj_ref[(3 * g + 1) * HD : (3 * g + 2) * HD, pl.ds(at, blk)]
                found.append(dot_nn(rows, grad_scores))
            return found

        def body(j, carry):
            found = blocks(pl.multiple_of(j * blk, blk), False)
            return tuple(a + b for a, b in zip(carry, found))

        grad_queries = lax.fori_loop(
            low_ref[i], own // blk + i, body, tuple(blocks(start, True))
        )
        for g in range(group):
            grad_proj[3 * g * HD : (3 * g + 1) * HD, start : start + blk] = (
                grad_queries[g] * (HD**-0.5)
            ).astype(low)

    for g in range(group):
        grad_proj[(3 * g + 1) * HD : (3 * g + 2) * HD, :] = grad_keys[g].astype(low)
        grad_proj[(3 * g + 2) * HD : (3 * g + 3) * HD, :] = grad_values[g].astype(low)


def attention_specs(group, own, seen):
    proj = pl.BlockSpec((group * 3 * HD, seen), lambda h, s: (h, 0))
    key_ids = pl.BlockSpec((seen, 1), lambda h, s: (0, 0))
    query_ids = pl.BlockSpec((1, own), lambda h, s: (0, 0))
    out = pl.BlockSpec((group * HD, own), lambda h, s: (h, 0))
    lse = pl.BlockSpec((group * 8, own), lambda h, s: (h, 0))
    return proj, key_ids, query_ids, out, lse


def attend_forward(proj, lows, key_ids, query_ids, blk):
    heads, seen = proj.shape[0] // (3 * HD), proj.shape[1]
    own = query_ids.shape[1]
    group = 2 if heads % 2 == 0 else 1
    proj_spec, key_spec, query_spec, out_spec, lse_spec = attention_specs(group, own, seen)
    return pl.pallas_call(
        partial(forward_kernel, blk, seen - own, group),
        out_shape=(
            jax.ShapeDtypeStruct((heads * HD, own), low),
            jax.ShapeDtypeStruct((heads * 8, own), full),
        ),
        grid_spec=pltpu.PrefetchScalarGridSpec(
            num_scalar_prefetch=1,
            grid=(heads // group,),
            in_specs=[proj_spec, key_spec, query_spec],
            out_specs=[out_spec, lse_spec],
            scratch_shapes=[pltpu.VMEM((group, seen, HD), low)],
        ),
        cost_estimate=pl.CostEstimate(
            flops=heads * own * 1024 * HD * 8,
            bytes_accessed=heads * HD * seen * 8,
            transcendentals=heads * own * 512,
        ),
        name="attend_forward",
    )(lows, proj, key_ids, query_ids)


def attend_backward(proj, lows, key_ids, query_ids, out, lse, grad, blk):
    heads, seen = proj.shape[0] // (3 * HD), proj.shape[1]
    own = query_ids.shape[1]
    group = 2 if heads % 2 == 0 else 1
    proj_spec, key_spec, query_spec, out_spec, lse_spec = attention_specs(group, own, seen)
    return pl.pallas_call(
        partial(backward_kernel, blk, seen - own, group),
        out_shape=jax.ShapeDtypeStruct(proj.shape, low),
        grid_spec=pltpu.PrefetchScalarGridSpec(
            num_scalar_prefetch=1,
            grid=(heads // group,),
            in_specs=[proj_spec, key_spec, query_spec, out_spec, lse_spec, out_spec],
            out_specs=proj_spec,
            scratch_shapes=[
                pltpu.VMEM((group, seen, HD), low),
                pltpu.VMEM((group, seen, HD), low),
                pltpu.VMEM((group, HD, seen), full),
                pltpu.VMEM((group, HD, seen), full),
            ],
        ),
        cost_estimate=pl.CostEstimate(
            flops=heads * own * 1024 * HD * 16,
            bytes_accessed=heads * HD * seen * 16,
            transcendentals=heads * own * 512,
        ),
        name="attend_backward",
    )(lows, proj, key_ids, query_ids, out, lse, grad)


def norm_forward(values):
    average = jnp.mean(values, axis=1, keepdims=True)
    square = jnp.mean(values * values, axis=1, keepdims=True)
    inverse = lax.rsqrt(square - average * average + epsilon)
    return (values - average) * inverse, inverse


def halves(array):
    middle = array.shape[0] // 2
    return array[:middle], array[middle:]


def per_device(
    tokens,
    segments,
    attend_gain,
    attend_shift,
    input_weight,
    input_bias,
    output_weight,
    output_bias,
    feed_gain,
    feed_shift,
    up_weight,
    up_bias,
    down_weight,
    down_bias,
    grad_out,
):
    row, col = lax.axis_index("row"), lax.axis_index("col")
    count = lax.axis_size("col")
    own, half = tokens.shape
    seqs, length = segments.shape
    blk = min(256, math.gcd(own, length))
    head_width = input_weight.shape[2]
    split_heads = head_width % (2 * HD) == 0
    first_core = row == 0
    order = distances(count)
    parts = order[: count // 2], order[count // 2 :]

    def mine_and_other(block):
        rows = block.shape[0] // 2
        block = block.reshape(2, rows, *block.shape[1:])
        return (
            lax.dynamic_index_in_dim(block, row, 0, False),
            lax.dynamic_index_in_dim(block, 1 - row, 0, False),
        )

    def by_core(kept, got):
        return jnp.concatenate(
            [jnp.where(first_core, kept, got), jnp.where(first_core, got, kept)], axis=0
        )

    def from_core(block):
        return by_core(block[:, :half], swap(block[:, half:]))

    def to_core(block):
        kept, sent = mine_and_other(block)
        return jnp.concatenate([kept, swap(sent)], axis=1)

    def from_other(block):
        block = block.astype(low)
        return swap(jnp.concatenate([block[:, half:], block[:, :half]], axis=1)).astype(full)

    def over_dp(block):
        if lax.axis_size("dp") == 2:
            block = block.astype(low)
            other = lax.ppermute(block, "dp", [(0, 1), (1, 0)])
            return block.astype(full) + other.astype(full)
        return lax.psum(block.astype(full), "dp")

    vectors = jnp.stack(
        [attend_gain, attend_shift, output_bias, feed_gain, feed_shift, down_bias]
    )
    labels = segments.astype(low).reshape(-1, half)
    small = jnp.concatenate([vectors, labels], axis=0)
    bias_up = mine_and_other(up_bias)[0]
    up_width = bias_up.shape[0]
    if split_heads:
        in_block = jnp.transpose(input_weight, (2, 1, 0))
        in_block = in_block.reshape(head_width // HD, HD, 3, half).transpose(0, 2, 1, 3)
        in_kept, in_sent = mine_and_other(in_block.reshape(3 * head_width, half))
        out_kept, out_sent = mine_and_other(output_weight)
        in_width, out_width = in_kept.shape[0], out_kept.shape[0]
        got = swap(jnp.concatenate([in_sent, out_sent, small], axis=0))
        weights = jnp.concatenate(
            [
                jnp.concatenate([in_kept, out_kept], axis=0),
                got[: in_width + out_width],
            ],
            axis=1,
        )
        other_small = got[in_width + out_width :]
        bias_in = input_bias.reshape(2, head_width // HD, HD)
        bias_in = jnp.stack([bias_in[0], jnp.zeros_like(bias_in[0]), bias_in[1]], axis=1)
        bias_in = mine_and_other(bias_in.reshape(-1))[0]
        bias_row = jnp.concatenate([bias_in, bias_up])
    else:
        in_width = out_width = 0
        weights = jnp.zeros((0, 2 * half), low)
        other_small = swap(small)
        bias_row = bias_up
    bias_rows = 32
    bias_row = jnp.pad(bias_row[None], ((0, bias_rows - 1), (0, 2 * half - bias_row.shape[0])))
    block = jnp.concatenate([weights, bias_row], axis=0)
    pieces = ring_gather(block, count)
    edges = [(0, in_width), (in_width, in_width + out_width)] if split_heads else []
    edges += [(in_width + out_width, in_width + out_width + bias_rows)]
    joined = [join(pieces, part, edges) for part in parts]
    last = pieces[count // 2 - 1][0][0]

    needs = [c for c in range(count) if (c * own) % length != 0]
    assert all((c * own) % length <= own for c in needs)
    halo = lax.ppermute(tokens, "col", [(c - 1, c) for c in needs])
    x_own = jnp.concatenate([tokens, swap(tokens)], axis=1).astype(full)
    x_halo = jnp.concatenate([halo, swap(halo)], axis=1).astype(full)
    vectors = jnp.concatenate([vectors, other_small[:6]], axis=1).astype(full)
    gain_one, shift_one, out_bias, gain_two, shift_two, _ = [vectors[k : k + 1] for k in range(6)]
    labels = by_core(labels, other_small[6:]).reshape(-1).astype(jnp.int32)
    places = jnp.arange(labels.shape[0], dtype=jnp.int32)
    idents = jnp.where(labels > 0, (places // length) * 4096 + labels, -1 - places)
    idents = jnp.concatenate([jnp.full((own,), -(2**30), jnp.int32), idents])
    idents = lax.dynamic_slice_in_dim(idents, col * own, 2 * own, 0)
    key_ids = idents[:, None]
    query_ids = idents[None, own:]
    heads_of_blocks = idents[own::blk]
    lows = jnp.argmax(idents[None, :] == heads_of_blocks[:, None], axis=1).astype(jnp.int32) // blk

    up_weight, down_weight = after((up_weight, down_weight), block)
    up_kept, up_sent = mine_and_other(jnp.transpose(up_weight))
    down_kept, down_sent = mine_and_other(down_weight)
    got = swap(jnp.concatenate([up_sent, down_sent], axis=0))
    up_block = jnp.concatenate([up_kept, got[:up_width]], axis=1)
    down_block = jnp.concatenate([down_kept, got[up_width:]], axis=1)
    up_pieces = ring_gather(after(up_block, last), count)
    last = up_pieces[count // 2 - 1][0][0]
    down_pieces = ring_gather(after(down_block, last), count)
    up = [join(up_pieces, part, [(0, up_width)])[0] for part in parts]
    down = [join(down_pieces, part, [(0, up_width)])[0] for part in parts]
    bias_rows_of = [v[-1].reshape(-1, bias_rows, 2 * half)[:, 0] for v in joined]
    if split_heads:
        into, out = [v[0] for v in joined], [v[1] for v in joined]
        bias_in = [v[:, :in_width].reshape(-1, 1).astype(full) for v in bias_rows_of]
        bias_up = [v[:, in_width : in_width + up_width] for v in bias_rows_of]
    else:
        heads = count * head_width // HD
        gathered = jnp.transpose(input_weight, (2, 1, 0))
        gathered = lax.all_gather(gathered, "col", axis=0, tiled=True)
        gathered = gathered.reshape(heads, HD, 3, half).transpose(0, 2, 1, 3)
        into = halves(to_core(gathered.reshape(heads * 3 * HD, half)))
        out = halves(to_core(lax.all_gather(output_weight, "col", axis=0, tiled=True)))
        bias_all = lax.all_gather(input_bias, "col", axis=1, tiled=True).reshape(2, heads, HD)
        bias_all = jnp.stack([bias_all[0], jnp.zeros_like(bias_all[0]), bias_all[1]], axis=1)
        bias_in = halves(mine_and_other(bias_all.reshape(-1, 1).astype(full))[0])
        bias_up = [v[:, :up_width] for v in bias_rows_of]
    bias_up = [v.reshape(1, -1).astype(full) for v in bias_up]

    both = range(2)
    near, far = 0, 1
    fixed = lax.optimization_barrier
    normed_one, inverse_one = norm_forward(x_own)
    normed_halo, _ = norm_forward(x_halo)
    first = jnp.concatenate([normed_halo, normed_one]) * gain_one + shift_one
    first = fixed(first.astype(low))
    proj, attended, lse = [], [], []
    for k in both:
        proj.append((dot_nt(into[k], first) + bias_in[k]).astype(low))
        result = attend_forward(proj[k], lows, key_ids, query_ids, blk)
        attended.append(result[0])
        lse.append(result[1])
    branch = sum(dot_tn(attended[k], out[k]) for k in both)
    middle = x_own + (branch + from_other(branch) + out_bias)
    normed_two, inverse_two = norm_forward(middle)
    second = fixed((normed_two * gain_two + shift_two).astype(low))
    hidden, slope = [], []
    for k in both:
        pre = dot_nt(second, up[k]) + bias_up[k]
        value, pull = jax.vjp(partial(jax.nn.gelu, approximate=True), pre)
        value, rate = fixed((value.astype(low), pull(jnp.ones_like(pre))[0]))
        hidden.append(value)
        slope.append(rate)
    grad_full = fixed(jnp.concatenate([grad_out, swap(grad_out)], axis=1))
    grad_down = [None, None]
    for k in (far, near):
        grad_down[k] = dot_tn(hidden[k], grad_full).astype(low)
    branch = sum(dot_nn(hidden[k], down[k]) for k in both)
    branch = branch[:, :half] + swap(branch[:, half:].astype(low)).astype(full)
    layer_out = (middle[:, :half] + (branch + down_bias.astype(full))).astype(low)

    grad_pre, grad_up, grad_up_bias = [None, None], [None, None], [None, None]
    for k in (far, near):
        grad_pre[k] = fixed((dot_nt(grad_full, down[k]) * slope[k]).astype(low))
        grad_up_bias[k] = jnp.sum(grad_pre[k].astype(full), axis=0)
        grad_up[k] = dot_tn(grad_pre[k], second).astype(low)
    grad_second = sum(dot_nn(grad_pre[k], up[k]) for k in both)
    grad_second = grad_second + from_other(grad_second)
    scaled = grad_second * gain_two
    grad_middle = grad_full.astype(full) + inverse_two * (
        scaled
        - jnp.mean(scaled, axis=1, keepdims=True)
        - normed_two * jnp.mean(scaled * normed_two, axis=1, keepdims=True)
    )
    grad_branch = fixed(grad_middle.astype(low))
    grad_output, grad_proj, grad_input = [None, None], [None, None], [None, None]
    grad_bias_in = [None, None]
    for k in (far, near):
        grad_output[k] = dot_nn(attended[k], grad_branch).astype(low)
    for k in (far, near):
        grad_attended = dot_nt(out[k], grad_branch).astype(low)
        grad_proj[k] = attend_backward(
            proj[k], lows, key_ids, query_ids, attended[k], lse[k], grad_attended, blk
        )
        grad_bias_in[k] = jnp.sum(grad_proj[k].astype(full), axis=1)
        grad_input[k] = dot_nn(grad_proj[k], first).astype(low)

    def split(blocks, unit):
        found = {}
        for part, block in zip(parts, blocks):
            for at, t in enumerate(part):
                found[t] = block[at * unit : (at + 1) * unit]
        return found

    def beside(*found):
        return {t: jnp.concatenate([f[t] for f in found], axis=0) for t in range(count)}

    total = ring_scatter(split(grad_down, up_width), count)
    grad_down_weight = over_dp(from_core(total.astype(low)))
    blocks = split(grad_up, up_width)
    if split_heads:
        blocks = beside(blocks, split(grad_output, out_width))
    total = from_core(ring_scatter(blocks, count).astype(low))
    total = over_dp(total).reshape(2, -1, half)
    grad_up_weight = jnp.transpose(total[:, :up_width].reshape(-1, half))
    grad_output_weight = total[:, up_width:].reshape(-1, half)

    rows = []
    for k in both:
        row_up = grad_up_bias[k].reshape(-1, up_width)
        if split_heads:
            row_up = jnp.concatenate([grad_bias_in[k].reshape(-1, in_width), row_up], axis=1)
        used = row_up.shape[1]
        row_up = jnp.pad(row_up[:, None], ((0, 0), (0, bias_rows - 1), (0, 2 * half - used)))
        rows.append(row_up.reshape(-1, 2 * half).astype(low))
    blocks = split(rows, bias_rows)
    if split_heads:
        blocks = beside(split(grad_input, in_width), blocks)
    total = ring_scatter(blocks, count).astype(low)
    bias_sums = total[in_width, : in_width + up_width]
    if split_heads:
        total = over_dp(from_core(total[:in_width]))
        total = total.reshape(head_width // HD, 3, HD, half)
        grad_input_weight = total.transpose(3, 1, 0, 2).reshape(half, 3, head_width)
    else:
        total = from_core(jnp.concatenate(grad_input)).reshape(heads, 3, HD, half)
        total = total.transpose(0, 2, 1, 3).reshape(heads * HD, 3, half).astype(full)
        total = lax.psum_scatter(total, "col", scatter_dimension=0, tiled=True)
        grad_input_weight = over_dp(total).transpose(2, 1, 0)
        total = from_core(jnp.concatenate(grad_output)).astype(full)
        total = lax.psum_scatter(total, "col", scatter_dimension=0, tiled=True)
        grad_output_weight = over_dp(total)
    bias_sums = over_dp(by_core(bias_sums[None], swap(bias_sums[None])))
    if split_heads:
        bias = bias_sums[:, :in_width].reshape(head_width // HD, 3, HD)
        grad_input_bias = jnp.stack([bias[:, 0].reshape(-1), bias[:, 2].reshape(-1)])
    else:
        bias = jnp.concatenate(grad_bias_in).reshape(heads // 2, 3, HD)
        bias = jnp.stack([bias[:, 0].reshape(-1), bias[:, 2].reshape(-1)], axis=1)
        bias = by_core(bias, swap(bias))
        bias = lax.psum_scatter(bias, "col", scatter_dimension=0, tiled=True)
        grad_input_bias = lax.psum(bias, "dp").T

    grad_first = sum(dot_tn(grad_proj[k], into[k]) for k in both)
    grad_first = grad_first[:, :half] + swap(grad_first[:, half:].astype(low)).astype(full)
    returned = lax.ppermute(grad_first[:own].astype(low), "col", [(c, c - 1) for c in needs])
    grad_first = grad_first[own:] + returned.astype(full)
    scaled = grad_first * gain_one[:, :half]
    normed_own = normed_one[:, :half]
    sums = jnp.concatenate(
        [
            jnp.sum(scaled, axis=1, keepdims=True),
            jnp.sum(scaled * normed_own, axis=1, keepdims=True),
        ],
        axis=1,
    )
    sums = (sums + swap(sums)) / (2 * half)
    grad_tokens = grad_middle[:, :half] + inverse_one * (
        scaled - sums[:, 0:1] - normed_own * sums[:, 1:2]
    )
    small = jnp.stack(
        [
            jnp.sum(grad_first * normed_own, axis=0),
            jnp.sum(grad_first, axis=0),
            jnp.sum(grad_branch[:, :half].astype(full), axis=0),
            jnp.sum(grad_second[:, :half] * normed_two[:, :half], axis=0),
            jnp.sum(grad_second[:, :half], axis=0),
            jnp.sum(grad_out.astype(full), axis=0),
        ]
    )
    small = sum_over(sum_over(small, "dp"), "col")
    return (
        layer_out,
        grad_tokens,
        small[0],
        small[1],
        grad_input_weight,
        grad_input_bias,
        grad_output_weight,
        small[2],
        small[3],
        small[4],
        grad_up_weight,
        bias_sums[:, in_width:].reshape(-1),
        grad_down_weight,
        small[5],
    )


def solution(mesh):
    in_specs = (
        P(("dp", "col"), "row"),
        P(("dp", "row"), None),
        P("row"),
        P("row"),
        P("row", None, "col"),
        P(None, "col"),
        P("col", "row"),
        P("row"),
        P("row"),
        P("row"),
        P("row", "col"),
        P("col"),
        P("col", "row"),
        P("row"),
        P(("dp", "col"), "row"),
    )
    out_specs = (
        P(("dp", "col"), "row"),
        P(("dp", "col"), "row"),
        P("row"),
        P("row"),
        P("row", None, "col"),
        P(None, "col"),
        P("col", "row"),
        P("row"),
        P("row"),
        P("row"),
        P("row", "col"),
        P("col"),
        P("col", "row"),
        P("row"),
    )
    return jax.shard_map(
        per_device, mesh=mesh, in_specs=in_specs, out_specs=out_specs, check_vma=False
    )
```

time: 655 us -> 528 us (0.81)
  blocking collectives: 73.4 us -> 0 us
  local copies, waits for them, and re-layouts: 89.3 us -> 47.1 us
  starting transfers between devices: 127 us -> 92.4 us
  waiting for transfers between devices: 168 us -> 152 us
  matrix products: 76.3 us -> 92.1 us
  other arithmetic: 61.6 us -> 74.3 us
  Pallas kernels: 46.3 us -> 57.6 us
    psum x1 -> x0, blocking collectives: 73.4 us -> none  [per_device(): small = lax.psum(small, ('dp', 'col'))]
    unnamed x265 -> x196, local copies, waits for them, and re-layouts: 63.3 us -> 18 us
    ppermute x84 -> x48, starting transfers between devices: 117 us -> 73.2 us  [shift(): return lax.ppermute(values, 'col', pairs)]
    ppermute x84 -> x48, waiting for transfers between devices: 157 us -> 136 us  [shift(): return lax.ppermute(values, 'col', pairs)]
    dot_general x4 -> x8, matrix products: 20.7 us -> 34.9 us  [dot_nn(): lax.dot_general(left, right, (((1,), (0,)), ((), ())), preferred_element_...]
    pallas_call x2 -> x10, Pallas kernels: 46.3 us -> 57.6 us  [the longest x2 20.6 us: attend_backward(): pl.pallas_call(partial(backward_kernel, blk, seen - own, group), out_shap...]
    ppermute x1, waiting for transfers between devices: 9.85 us -> 0.01 us  [per_device(): lax.ppermute(grad_first[:own].astype(low), 'col', [(c, c - 1) for c in ne...]
    reduce_sum x5 -> x8, other arithmetic: 3.94 us -> 12.9 us  [the longest x2 4.1 us: per_device(): grad_bias_in[k] = jnp.sum(grad_proj[k].astype(full), axis=1)]
  transfers between devices with their start and end apart: 108 -> 72, of which waited for: 51 -> 27; matrix products, arithmetic and copies ran while one was open for 26% -> 38% of each run, Pallas kernels for 7% -> 11%
where the time goes in v2:
time: 528 us; the launch traced here: 518 us
  waiting for transfers between devices  152 us (29%)
  starting transfers between devices  92.4 us (18%)
  matrix products  92.1 us (17%)
  other arithmetic  74.3 us (14%)
  Pallas kernels  57.6 us (11%)
  local copies, waits for them, and re-layouts  47.1 us (9%)
    ppermute x48, waiting for transfers between devices, shift(): return lax.ppermute(values, 'col', pairs)  136 us
    ppermute x48, starting transfers between devices, shift(): return lax.ppermute(values, 'col', pairs)  73.2 us
    dot_general x8, matrix products, dot_nn(): lax.dot_general(left, right, (((1,), (0,)), ((), ())), preferred_element_...  34.9 us
    dot_general x8, matrix products, dot_nt(): lax.dot_general(left, right, (((1,), (1,)), ((), ())), preferred_element_...  30.1 us
    dot_general x8, matrix products, dot_tn(): lax.dot_general(left, right, (((0,), (0,)), ((), ())), preferred_element_...  27.1 us
    pallas_call x2, Pallas kernels, attend_backward(): pl.pallas_call(partial(backward_kernel, blk, seen - own, group), out_shap...  20.6 us
    pallas_call x2, Pallas kernels, attend_forward(): pl.pallas_call(partial(forward_kernel, blk, seen - own, group), out_shape...  19 us
    unnamed x196, local copies, waits for them, and re-layouts  18 us
  transfers between devices with their start and end apart: 72, of which 27 were waited for; matrix products, arithmetic and copies ran while one was open for 38% of the time, Pallas kernels for 11%

profile of v2, /device:TPU:0, one launch (start us, length us, event | category | flops | bytes accessed | tf_op | source)
XLA Modules:
  0.0 518.5 jit_solution(9547228344024342996)
XLA Ops:
  1.3 5.5 %collective-permute-start.5 = (bf16[768,512]{1,0:T(8,128)(2,1)}, bf16[768,512]{1,0:T(8,128)(2,1)}, u32[]{:S(2)}, u32[]{:S(2)}) collective-permute-start(bf16[768,512]{1,0:T(8,128)(2,1)} %param.15), channel_id=1, source_target_pairs={{0,1},{1,2},{2,3},{4,5},{5,6},{6,7},{8,9},{9,10},{10,11},{12,13},{... | collective-permute-start | bytes 2359304 | tf_op jit(solution)/shard_map/ppermute | solution.py:460
  18.3 5.8 %collective-permute-done.5 = bf16[768,512]{1,0:T(8,128)(2,1)} collective-permute-done((bf16[768,512]{1,0:T(8,128)(2,1)}, bf16[768,512]{1,0:T(8,128)(2,1)}, u32[]{:S(2)}, u32[]{:S(2)}) %collective-permute-start.5) | collective-permute-done | bytes 786464 | tf_op jit(solution)/shard_map/ppermute | solution.py:460
  30.0 6.1 %collective-permute-done.3.refs_2_ = bf16[288,1024]{1,0:T(8,128)(2,1)} collective-permute-done((bf16[288,1024]{1,0:T(8,128)(2,1)}, bf16[288,1024]{1,0:T(8,128)(2,1)}, u32[]{:S(2)}, u32[]{:S(2)}) %collective-permute-start.3) | collective-permute-done | bytes 589856 | tf_op jit(solution)/shard_map/ppermute | solution.py:47
  41.7 3.0 join.6
  48.2 3.0 collective-permute-done.7.refs_0_
  60.1 4.0 add_convert_fusion.1.proj_ref
  64.0 9.5 %attend_forward.2 = (bf16[256,768]{1,0:T(8,128)(2,1)}, f32[32,768]{1,0:T(8,128)}) custom-call(s32[3]{0:T(128)} %and_select_fusion.low_ref, bf16[768,1536]{1,0:T(8,128)(2,1)} %add_convert_fusion.1.proj_ref, s32[1536,1]{1,0:T(8,128)} %broadcast_in_dim.42.key_ids, s32[1,768]{1,0:T(1,128)} %broadcast_in_dim.18.query_ids), custom_call_target="tpu_custom_call" | custom-call | flops 1610612736 | bytes 3145728 | tf_op jit(solution)/shard_map/attend_forward/pallas_call | solution.py:296
  74.5 5.1 collective-permute-start.10
  80.7 3.6 fusion.65
  89.5 3.0 join.7
  93.4 5.4 %add_convert_fusion.proj_ref = bf16[768,1536]{1,0:T(8,128)(2,1)} fusion(bf16[768,1024]{1,0:T(8,128)(2,1)} %get-tuple-element.38, bf16[1536,1024]{1,0:T(8,128)(2,1)S(1)} %copy-done.18, f32[768]{0:T(1024)S(1)} %reshape.235), kind=kOutput, calls=%fused_computation.10 | convolution fusion | flops 2418278400 | bytes 7080960 | tf_op jit(solution)/shard_map/dot_general | solution.py:24
  98.9 9.5 %attend_forward.3 = (bf16[256,768]{1,0:T(8,128)(2,1)}, f32[32,768]{1,0:T(8,128)}) custom-call(s32[3]{0:T(128)} %and_select_fusion.low_ref, bf16[768,1536]{1,0:T(8,128)(2,1)} %add_convert_fusion.proj_ref, s32[1536,1]{1,0:T(8,128)} %broadcast_in_dim.42.key_ids, s32[1,768]{1,0:T(1,128)} %broadcast_in_dim.18.query_ids), custom_call_target="tpu_custom_call" | custom-call | flops 1610612736 | bytes 3145728 | tf_op jit(solution)/shard_map/attend_forward/pallas_call | solution.py:296
  112.7 3.5 collective-permute-start.16
  116.4 11.9 %collective-permute-done.16.refs_3_ = bf16[256,1024]{1,0:T(8,128)(2,1)S(1)} collective-permute-done((bf16[256,1024]{1,0:T(8,128)(2,1)}, bf16[256,1024]{1,0:T(8,128)(2,1)S(1)}, u32[]{:S(2)}, u32[]{:S(2)}) %collective-permute-start.16) | collective-permute-done | bytes 524320 | tf_op jit(solution)/shard_map/ppermute | solution.py:47
  135.3 8.9 %collective-permute-done.17.refs_1_ = bf16[256,1024]{1,0:T(8,128)(2,1)S(1)} collective-permute-done((bf16[256,1024]{1,0:T(8,128)(2,1)S(1)}, bf16[256,1024]{1,0:T(8,128)(2,1)S(1)}, u32[]{:S(2)}, u32[]{:S(2)}) %collective-permute-start.17) | collective-permute-done | bytes 524320 | tf_op jit(solution)/shard_map/ppermute | solution.py:47
  149.4 3.0 join.8
  155.9 3.0 join.10
  164.7 5.0 fusion.13
  169.7 5.0 fusion.7
  179.7 3.2 convolution_convert_fusion.1
  190.3 7.0 %collective-permute-done.20.refs_3_ = bf16[256,1024]{1,0:T(8,128)(2,1)} collective-permute-done((bf16[256,1024]{1,0:T(8,128)(2,1)}, bf16[256,1024]{1,0:T(8,128)(2,1)}, u32[]{:S(2)}, u32[]{:S(2)}) %collective-permute-start.20) | collective-permute-done | bytes 524320 | tf_op jit(solution)/shard_map/ppermute | solution.py:47
  197.3 3.0 join.9
  200.3 4.9 multiply_convert_fusion.1
  209.2 3.4 fusion.66
  218.8 5.6 %fusion.67 = f32[768,1024]{1,0:T(8,128)} fusion(bf16[768,1024]{1,0:T(8,128)(2,1)} %copy-done.44, bf16[1024,1024]{1,0:T(8,128)(2,1)} %join.8), kind=kOutput, calls=%fused_computation.242 | convolution fusion | flops 1610612736 | bytes 6815744 | tf_op jit(solution)/shard_map/dot_general | solution.py:20
  228.5 3.8 collective-permute-done.64
  238.5 2.9 join.11
  241.4 4.9 convolution_add_fusion.3
  249.0 3.0 multiply_convert_fusion
  253.7 6.4 %fusion.64 = (bf16[768,1024]{1,0:T(8,128)(2,1)S(1)}, f32[768,1024]{1,0:T(8,128)}) fusion(f32[768,1024]{1,0:T(8,128)} %fusion.67, bf16[768,1024]{1,0:T(8,128)(2,1)} %multiply_convert_fusion, bf16[1024,1024]{1,0:T(8,128)(2,1)} %join.10), kind=kOutput, calls=%fused_computation.239 | convolution fusion | flops 1612185600 | bytes 11534336 | tf_op jit(solution)/shard_map/dot_general | solution.py:20
  262.2 3.9 convolution_convert_fusion.2
  271.7 4.7 collective-permute-done.52
  277.3 5.7 %collective-permute-done.69 = bf16[256,1024]{1,0:T(8,128)(2,1)S(1)} collective-permute-done((bf16[256,1024]{1,0:T(8,128)(2,1)S(1)}, bf16[256,1024]{1,0:T(8,128)(2,1)S(1)}, u32[]{:S(2)}, u32[]{:S(2)}) %collective-permute-start.69) | collective-permute-done | bytes 524320 | tf_op jit(solution)/shard_map/ppermute | solution.py:47
  297.5 10.2 %attend_backward.3 = bf16[768,1536]{1,0:T(8,128)(2,1)} custom-call(s32[3]{0:T(128)} %and_select_fusion.low_ref, bf16[768,1536]{1,0:T(8,128)(2,1)} %add_convert_fusion.proj_ref, s32[1536,1]{1,0:T(8,128)} %broadcast_in_dim.42.key_ids, s32[1,768]{1,0:T(1,128)} %broadcast_in_dim.18.query_ids, bf16[256,768]{1,0:T(8,128)(2,1)} %get-tuple-element.40.out_ref, ...), custom_call_target="tpu_custom_call" | custom-call | flops 3221225472 | bytes 6291456 | tf_op jit(solution)/shard_map/attend_backward/pallas_call | solution.py:323
  309.7 5.2 %convolution_convert_fusion.4 = bf16[768,1024]{1,0:T(8,128)(2,1)S(1)} fusion(bf16[768,1536]{1,0:T(8,128)(2,1)} %attend_backward.3, bf16[1536,1024]{1,0:T(8,128)(2,1)} %copy-done.17), kind=kOutput, calls=%fused_computation.53 | convolution fusion | flops 2416705536 | bytes 7077888 | tf_op jit(solution)/shard_map/dot_general | solution.py:20
  317.4 10.4 %attend_backward.2 = bf16[768,1536]{1,0:T(8,128)(2,1)} custom-call(s32[3]{0:T(128)} %and_select_fusion.low_ref, bf16[768,1536]{1,0:T(8,128)(2,1)} %add_convert_fusion.1.proj_ref, s32[1536,1]{1,0:T(8,128)} %broadcast_in_dim.42.key_ids, s32[1,768]{1,0:T(1,128)} %broadcast_in_dim.18.query_ids, bf16[256,768]{1,0:T(8,128)(2,1)} %get-tuple-element.36.out_ref, ...), custom_call_target="tpu_custom_call" | custom-call | flops 3221225472 | bytes 6291456 | tf_op jit(solution)/shard_map/attend_backward/pallas_call | solution.py:323
  327.8 7.4 %fusion.68 = f32[1536,1024]{1,0:T(8,128)} fusion(bf16[768,1536]{1,0:T(8,128)(2,1)} %attend_backward.2, bf16[768,1024]{1,0:T(8,128)(2,1)} %get-tuple-element.34), kind=kOutput, calls=%fused_computation.243 | convolution fusion | flops 2415919104 | bytes 10223616 | tf_op jit(solution)/shard_map/dot_general | solution.py:28
  337.2 6.5 %convolution_convert_fusion.5 = bf16[768,1024]{1,0:T(8,128)(2,1)} fusion(bf16[768,1536]{1,0:T(8,128)(2,1)} %attend_backward.2, bf16[1536,1024]{1,0:T(8,128)(2,1)} %copy-done.17), kind=kOutput, calls=%fused_computation.54 | convolution fusion | flops 2416705536 | bytes 7077888 | tf_op jit(solution)/shard_map/dot_general | solution.py:20
  362.0 4.3 collective-permute-start.56
  376.0 7.9 %collective-permute-done.45 = bf16[224,1024]{1,0:T(8,128)(2,1)S(1)} collective-permute-done((bf16[224,1024]{1,0:T(8,128)(2,1)S(1)}, bf16[224,1024]{1,0:T(8,128)(2,1)S(1)}, u32[]{:S(2)}, u32[]{:S(2)}) %collective-permute-start.45) | collective-permute-done | bytes 458784 | tf_op jit(solution)/shard_map/ppermute | solution.py:47
  386.8 9.0 %collective-permute-done.41 = bf16[224,1024]{1,0:T(8,128)(2,1)S(1)} collective-permute-done((bf16[224,1024]{1,0:T(8,128)(2,1)S(1)}, bf16[224,1024]{1,0:T(8,128)(2,1)S(1)}, u32[]{:S(2)}, u32[]{:S(2)}) %collective-permute-start.41) | collective-permute-done | bytes 458784 | tf_op jit(solution)/shard_map/ppermute | solution.py:47
  398.3 11.8 %collective-permute-done.46 = bf16[224,1024]{1,0:T(8,128)(2,1)S(1)} collective-permute-done((bf16[224,1024]{1,0:T(8,128)(2,1)S(1)}, bf16[224,1024]{1,0:T(8,128)(2,1)S(1)}, u32[]{:S(2)}, u32[]{:S(2)}) %collective-permute-start.46) | collective-permute-done | bytes 458784 | tf_op jit(solution)/shard_map/ppermute | solution.py:47
  418.4 6.0 %collective-permute-done.47 = bf16[224,1024]{1,0:T(8,128)(2,1)S(1)} collective-permute-done((bf16[224,1024]{1,0:T(8,128)(2,1)S(1)}, bf16[224,1024]{1,0:T(8,128)(2,1)S(1)}, u32[]{:S(2)}, u32[]{:S(2)}) %collective-permute-start.47) | collective-permute-done | bytes 458784 | tf_op jit(solution)/shard_map/ppermute | solution.py:47
  424.5 11.4 %collective-permute-done.43 = bf16[224,1024]{1,0:T(8,128)(2,1)S(1)} collective-permute-done((bf16[224,1024]{1,0:T(8,128)(2,1)S(1)}, bf16[224,1024]{1,0:T(8,128)(2,1)S(1)}, u32[]{:S(2)}, u32[]{:S(2)}) %collective-permute-start.43) | collective-permute-done | bytes 458784 | tf_op jit(solution)/shard_map/ppermute | solution.py:47
  452.4 3.3 collective-permute-done.55
  455.7 24.7 %collective-permute-done.59 = bf16[320,1024]{1,0:T(8,128)(2,1)} collective-permute-done((bf16[320,1024]{1,0:T(8,128)(2,1)}, bf16[320,1024]{1,0:T(8,128)(2,1)}, u32[]{:S(2)}, u32[]{:S(2)}) %collective-permute-start.59) | collective-permute-done | bytes 655392 | tf_op jit(solution)/shard_map/ppermute | solution.py:47
  505.9 3.7 slice_add_fusion.2
  510.2 5.5 %collective-permute-done.61 = bf16[640,512]{1,0:T(8,128)(2,1)S(1)} collective-permute-done((bf16[640,512]{1,0:T(8,128)(2,1)S(1)}, bf16[640,512]{1,0:T(8,128)(2,1)S(1)}, u32[]{:S(2)}, u32[]{:S(2)}) %collective-permute-start.61) | collective-permute-done | bytes 655392 | tf_op jit(solution)/shard_map/ppermute | solution.py:414
  (504 shorter events, 222.1 us)
Async XLA Ops:
  0.8 23.4 %collective-permute-start = (bf16[768,512]{1,0:T(8,128)(2,1)}, bf16[768,512]{1,0:T(8,128)(2,1)S(1)}, u32[]{:S(2)}, u32[]{:S(2)}) collective-permute-start(bf16[768,512]{1,0:T(8,128)(2,1)} %param.15), channel_id=1, source_target_pairs={{0,8},{8,0},{1,9},{9,1},{2,10},{10,2},{3,11},{11,3},{4,12},{12,4},... | collective-permute-start | bytes 2359304 | tf_op jit(solution)/shard_map/ppermute | solution.py:146
  1.3 22.8 %collective-permute-start.5 = (bf16[768,512]{1,0:T(8,128)(2,1)}, bf16[768,512]{1,0:T(8,128)(2,1)}, u32[]{:S(2)}, u32[]{:S(2)}) collective-permute-start(bf16[768,512]{1,0:T(8,128)(2,1)} %param.15), channel_id=1, source_target_pairs={{0,1},{1,2},{2,3},{4,5},{5,6},{6,7},{8,9},{9,10},{10,11},{12,13},{... | collective-permute-start | bytes 2359304 | tf_op jit(solution)/shard_map/ppermute | solution.py:460
  11.0 15.7 %collective-permute-start.2 = (bf16[288,1024]{1,0:T(8,128)(2,1)}, bf16[288,1024]{1,0:T(8,128)(2,1)}, u32[]{:S(2)}, u32[]{:S(2)}) collective-permute-start(bf16[288,1024]{1,0:T(8,128)(2,1)} %fusion.27.refs_0_), channel_id=1, source_target_pairs={{0,2},{2,4},{4,6},{6,7},{7,5},{5,3},{3,1},{1,0},{8,10},{10,12},{12... | collective-permute-start | bytes 1769480 | tf_op jit(solution)/shard_map/ppermute | solution.py:47
  11.7 24.4 %collective-permute-start.3 = (bf16[288,1024]{1,0:T(8,128)(2,1)}, bf16[288,1024]{1,0:T(8,128)(2,1)}, u32[]{:S(2)}, u32[]{:S(2)}) collective-permute-start(bf16[288,1024]{1,0:T(8,128)(2,1)} %fusion.27.refs_0_), channel_id=1, source_target_pairs={{2,0},{4,2},{6,4},{7,6},{5,7},{3,5},{1,3},{0,1},{10,8},{12,10},{14... | collective-permute-start | bytes 1769480 | tf_op jit(solution)/shard_map/ppermute | solution.py:47
  17.0 21.6 %collective-permute-start.13 = (bf16[512,512]{1,0:T(8,128)(2,1)}, bf16[512,512]{1,0:T(8,128)(2,1)S(1)}, u32[]{:S(2)}, u32[]{:S(2)}) collective-permute-start(bf16[512,512]{1,0:T(8,128)(2,1)} %pad_maximum_fusion.7), channel_id=1, source_target_pairs={{0,8},{8,0},{1,9},{9,1},{2,10},{10,2},{3,11},{11,3},{4,12},{12,4},... | collective-permute-start | bytes 1572872 | tf_op jit(solution)/shard_map/ppermute | solution.py:146
  24.1 29.6 %collective-permute-start.6 = (bf16[768,512]{1,0:T(8,128)(2,1)}, bf16[768,512]{1,0:T(8,128)(2,1)}, u32[]{:S(2)}, u32[]{:S(2)}) collective-permute-start(bf16[768,512]{1,0:T(8,128)(2,1)} %collective-permute-done.5), channel_id=1, source_target_pairs={{0,8},{8,0},{1,9},{9,1},{2,10},{10,2},{3,11},{11,3},{4,12},{12,4},... | collective-permute-start | bytes 2359304 | tf_op jit(solution)/shard_map/ppermute | solution.py:146
  26.7 15.0 %collective-permute-start.4 = (bf16[288,1024]{1,0:T(8,128)(2,1)}, bf16[288,1024]{1,0:T(8,128)(2,1)}, u32[]{:S(2)}, u32[]{:S(2)}) collective-permute-start(bf16[288,1024]{1,0:T(8,128)(2,1)} %collective-permute-done.2.refs_1_), channel_id=1, source_target_pairs={{0,2},{2,4},{4,6},{6,7},{7,5},{5,3},{3,1},{1,0},{8,10},{10,12},{12... | collective-permute-start | bytes 1769480 | tf_op jit(solution)/shard_map/ppermute | solution.py:47
  36.1 15.0 %collective-permute-start.7 = (bf16[288,1024]{1,0:T(8,128)(2,1)}, bf16[288,1024]{1,0:T(8,128)(2,1)}, u32[]{:S(2)}, u32[]{:S(2)}) collective-permute-start(bf16[288,1024]{1,0:T(8,128)(2,1)} %collective-permute-done.3.refs_2_), channel_id=1, source_target_pairs={{2,0},{4,2},{6,4},{7,6},{5,7},{3,5},{1,3},{0,1},{10,8},{12,10},{14... | collective-permute-start | bytes 1769480 | tf_op jit(solution)/shard_map/ppermute | solution.py:47
  45.7 27.8 %collective-permute-start.8 = (bf16[288,1024]{1,0:T(8,128)(2,1)}, bf16[288,1024]{1,0:T(8,128)(2,1)}, u32[]{:S(2)}, u32[]{:S(2)}) collective-permute-start(bf16[288,1024]{1,0:T(8,128)(2,1)} %collective-permute-done.4.refs_3_), channel_id=1, source_target_pairs={{0,2},{2,4},{4,6},{6,7},{7,5},{5,3},{3,1},{1,0},{8,10},{10,12},{12... | collective-permute-start | bytes 1769480 | tf_op jit(solution)/shard_map/ppermute | solution.py:47
  51.2 28.5 %collective-permute-start.9 = (bf16[288,1024]{1,0:T(8,128)(2,1)}, bf16[288,1024]{1,0:T(8,128)(2,1)}, u32[]{:S(2)}, u32[]{:S(2)}) collective-permute-start(bf16[288,1024]{1,0:T(8,128)(2,1)} %collective-permute-done.7.refs_0_), channel_id=1, source_target_pairs={{2,0},{4,2},{6,4},{7,6},{5,7},{3,5},{1,3},{0,1},{10,8},{12,10},{14... | collective-permute-start | bytes 1769480 | tf_op jit(solution)/shard_map/ppermute | solution.py:47
  74.5 14.9 %collective-permute-start.10 = (bf16[144,1024]{1,0:T(8,128)(2,1)S(1)}, bf16[144,1024]{1,0:T(8,128)(2,1)}, u32[]{:S(2)}, u32[]{:S(2)}) collective-permute-start(bf16[144,1024]{1,0:T(8,128)(2,1)S(1)} %slice.541), channel_id=1, source_target_pairs={{0,2},{2,4},{4,6},{6,7},{7,5},{5,3},{3,1},{1,0},{8,10},{10,12},{12... | collective-permute-start | bytes 884744 | tf_op jit(solution)/shard_map/ppermute | solution.py:47
  84.3 28.3 %collective-permute-start.14 = (bf16[256,1024]{1,0:T(8,128)(2,1)}, bf16[256,1024]{1,0:T(8,128)(2,1)}, u32[]{:S(2)}, u32[]{:S(2)}) collective-permute-start(bf16[256,1024]{1,0:T(8,128)(2,1)} %pad_maximum_fusion.8.refs_0_), channel_id=1, source_target_pairs={{0,2},{2,4},{4,6},{6,7},{7,5},{5,3},{3,1},{1,0},{8,10},{10,12},{12... | collective-permute-start | bytes 1572872 | tf_op jit(solution)/shard_map/ppermute | solution.py:47
  86.8 29.3 %collective-permute-start.15 = (bf16[256,1024]{1,0:T(8,128)(2,1)}, bf16[256,1024]{1,0:T(8,128)(2,1)}, u32[]{:S(2)}, u32[]{:S(2)}) collective-permute-start(bf16[256,1024]{1,0:T(8,128)(2,1)} %pad_maximum_fusion.8.refs_0_), channel_id=1, source_target_pairs={{2,0},{4,2},{6,4},{7,6},{5,7},{3,5},{1,3},{0,1},{10,8},{12,10},{14... | collective-permute-start | bytes 1572872 | tf_op jit(solution)/shard_map/ppermute | solution.py:47
  112.7 46.3 %collective-permute-start.12 = (bf16[768,1024]{1,0:T(8,128)(2,1)}, bf16[768,1024]{1,0:T(8,128)(2,1)}, u32[]{:S(2)}, u32[]{:S(2)}) collective-permute-start(bf16[768,1024]{1,0:T(8,128)(2,1)} %pad_maximum_fusion.2), channel_id=1, source_target_pairs={{0,8},{8,0},{1,9},{9,1},{2,10},{10,2},{3,11},{11,3},{4,12},{12,4},... | collective-permute-start | bytes 4718600 | tf_op jit(solution)/shard_map/ppermute | solution.py:146
  112.7 15.6 %collective-permute-start.16 = (bf16[256,1024]{1,0:T(8,128)(2,1)}, bf16[256,1024]{1,0:T(8,128)(2,1)S(1)}, u32[]{:S(2)}, u32[]{:S(2)}) collective-permute-start(bf16[256,1024]{1,0:T(8,128)(2,1)} %collective-permute-done.14.refs_1_), channel_id=1, source_target_pairs={{0,2},{2,4},{4,6},{6,7},{7,5},{5,3},{3,1},{1,0},{8,10},{10,12},{12... | collective-permute-start | bytes 1572872 | tf_op jit(solution)/shard_map/ppermute | solution.py:47
  116.2 14.5 %collective-permute-start.21 = (bf16[256,1024]{1,0:T(8,128)(2,1)}, bf16[256,1024]{1,0:T(8,128)(2,1)S(1)}, u32[]{:S(2)}, u32[]{:S(2)}) collective-permute-start(bf16[256,1024]{1,0:T(8,128)(2,1)} %collective-permute-done.15.refs_2_), channel_id=1, source_target_pairs={{2,0},{4,2},{6,4},{7,6},{5,7},{3,5},{1,3},{0,1},{10,8},{12,10},{14... | collective-permute-start | bytes 1572872 | tf_op jit(solution)/shard_map/ppermute | solution.py:47
  116.2 16.9 %collective-permute-start.31 = (bf16[768,512]{1,0:T(8,128)(2,1)S(1)}, bf16[768,512]{1,0:T(8,128)(2,1)S(1)}, u32[]{:S(2)}, u32[]{:S(2)}) collective-permute-start(bf16[768,512]{1,0:T(8,128)(2,1)S(1)} %copy-done.16), channel_id=1, source_target_pairs={{0,8},{8,0},{1,9},{9,1},{2,10},{10,2},{3,11},{11,3},{4,12},{12,4},... | collective-permute-start | bytes 2359304 | tf_op jit(solution)/shard_map/ppermute | solution.py:146
  128.3 15.9 %collective-permute-start.17 = (bf16[256,1024]{1,0:T(8,128)(2,1)S(1)}, bf16[256,1024]{1,0:T(8,128)(2,1)S(1)}, u32[]{:S(2)}, u32[]{:S(2)}) collective-permute-start(bf16[256,1024]{1,0:T(8,128)(2,1)S(1)} %collective-permute-done.16.refs_3_), channel_id=1, source_target_pairs={{0,2},{2,4},{4,6},{6,7},{7,5},{5,3},{3,1},{1,0},{8,10},{10,12},{12... | collective-permute-start | bytes 1572872 | tf_op jit(solution)/shard_map/ppermute | solution.py:47
  130.7 15.1 %collective-permute-start.22 = (bf16[256,1024]{1,0:T(8,128)(2,1)S(1)}, bf16[256,1024]{1,0:T(8,128)(2,1)S(1)}, u32[]{:S(2)}, u32[]{:S(2)}) collective-permute-start(bf16[256,1024]{1,0:T(8,128)(2,1)S(1)} %collective-permute-done.21.refs_0_), channel_id=1, source_target_pairs={{2,0},{4,2},{6,4},{7,6},{5,7},{3,5},{1,3},{0,1},{10,8},{12,10},{14... | collective-permute-start | bytes 1572872 | tf_op jit(solution)/shard_map/ppermute | solution.py:47
  152.4 26.4 %collective-permute-start.18 = (bf16[256,1024]{1,0:T(8,128)(2,1)}, bf16[256,1024]{1,0:T(8,128)(2,1)}, u32[]{:S(2)}, u32[]{:S(2)}) collective-permute-start(bf16[256,1024]{1,0:T(8,128)(2,1)} %pad_maximum_fusion.9.refs_0_), channel_id=1, source_target_pairs={{0,2},{2,4},{4,6},{6,7},{7,5},{5,3},{3,1},{1,0},{8,10},{10,12},{12... | collective-permute-start | bytes 1572872 | tf_op jit(solution)/shard_map/ppermute | solution.py:47
  152.4 30.5 %collective-permute-start.19 = (bf16[256,1024]{1,0:T(8,128)(2,1)}, bf16[256,1024]{1,0:T(8,128)(2,1)}, u32[]{:S(2)}, u32[]{:S(2)}) collective-permute-start(bf16[256,1024]{1,0:T(8,128)(2,1)} %pad_maximum_fusion.9.refs_0_), channel_id=1, source_target_pairs={{2,0},{4,2},{6,4},{7,6},{5,7},{3,5},{1,3},{0,1},{10,8},{12,10},{14... | collective-permute-start | bytes 1572872 | tf_op jit(solution)/shard_map/ppermute | solution.py:47
  178.8 18.5 %collective-permute-start.20 = (bf16[256,1024]{1,0:T(8,128)(2,1)}, bf16[256,1024]{1,0:T(8,128)(2,1)}, u32[]{:S(2)}, u32[]{:S(2)}) collective-permute-start(bf16[256,1024]{1,0:T(8,128)(2,1)} %collective-permute-done.18.refs_1_), channel_id=1, source_target_pairs={{0,2},{2,4},{4,6},{6,7},{7,5},{5,3},{3,1},{1,0},{8,10},{10,12},{12... | collective-permute-start | bytes 1572872 | tf_op jit(solution)/shard_map/ppermute | solution.py:47
  182.9 25.1 %collective-permute-start.25 = (bf16[256,1024]{1,0:T(8,128)(2,1)}, bf16[256,1024]{1,0:T(8,128)(2,1)}, u32[]{:S(2)}, u32[]{:S(2)}) collective-permute-start(bf16[256,1024]{1,0:T(8,128)(2,1)} %collective-permute-done.19.refs_2_), channel_id=1, source_target_pairs={{2,0},{4,2},{6,4},{7,6},{5,7},{3,5},{1,3},{0,1},{10,8},{12,10},{14... | collective-permute-start | bytes 1572872 | tf_op jit(solution)/shard_map/ppermute | solution.py:47
  187.2 25.4 %collective-permute-start.63 = (bf16[256,1024]{1,0:T(8,128)(2,1)}, bf16[256,1024]{1,0:T(8,128)(2,1)}, u32[]{:S(2)}, u32[]{:S(2)}) collective-permute-start(bf16[256,1024]{1,0:T(8,128)(2,1)} %pad_maximum_fusion.10), channel_id=1, source_target_pairs={{0,2},{2,4},{4,6},{6,7},{7,5},{5,3},{3,1},{1,0},{8,10},{10,12},{12... | collective-permute-start | bytes 1572872 | tf_op jit(solution)/shard_map/ppermute | solution.py:47
  189.7 38.7 %collective-permute-start.67 = (bf16[256,1024]{1,0:T(8,128)(2,1)}, bf16[256,1024]{1,0:T(8,128)(2,1)}, u32[]{:S(2)}, u32[]{:S(2)}) collective-permute-start(bf16[256,1024]{1,0:T(8,128)(2,1)} %pad_maximum_fusion.11), channel_id=1, source_target_pairs={{2,0},{4,2},{6,4},{7,6},{5,7},{3,5},{1,3},{0,1},{10,8},{12,10},{14... | collective-permute-start | bytes 1572872 | tf_op jit(solution)/shard_map/ppermute | solution.py:47
  207.1 17.3 %collective-permute-start.26 = (bf16[256,1024]{1,0:T(8,128)(2,1)}, bf16[256,1024]{1,0:T(8,128)(2,1)}, u32[]{:S(2)}, u32[]{:S(2)}) collective-permute-start(bf16[256,1024]{1,0:T(8,128)(2,1)} %collective-permute-done.20.refs_3_), channel_id=1, source_target_pairs={{0,2},{2,4},{4,6},{6,7},{7,5},{5,3},{3,1},{1,0},{8,10},{10,12},{12... | collective-permute-start | bytes 1572872 | tf_op jit(solution)/shard_map/ppermute | solution.py:47
  208.1 19.0 %collective-permute-start.27 = (bf16[256,1024]{1,0:T(8,128)(2,1)}, bf16[256,1024]{1,0:T(8,128)(2,1)}, u32[]{:S(2)}, u32[]{:S(2)}) collective-permute-start(bf16[256,1024]{1,0:T(8,128)(2,1)} %collective-permute-done.25.refs_0_), channel_id=1, source_target_pairs={{2,0},{4,2},{6,4},{7,6},{5,7},{3,5},{1,3},{0,1},{10,8},{12,10},{14... | collective-permute-start | bytes 1572872 | tf_op jit(solution)/shard_map/ppermute | solution.py:47
  214.8 17.5 %collective-permute-start.64 = (bf16[256,1024]{1,0:T(8,128)(2,1)}, bf16[256,1024]{1,0:T(8,128)(2,1)}, u32[]{:S(2)}, u32[]{:S(2)}) collective-permute-start(bf16[256,1024]{1,0:T(8,128)(2,1)} %add_convert_fusion.12), channel_id=1, source_target_pairs={{0,2},{2,4},{4,6},{6,7},{7,5},{5,3},{3,1},{1,0},{8,10},{10,12},{12... | collective-permute-start | bytes 1572872 | tf_op jit(solution)/shard_map/ppermute | solution.py:47
  234.8 32.3 %collective-permute-start.68 = (bf16[256,1024]{1,0:T(8,128)(2,1)}, bf16[256,1024]{1,0:T(8,128)(2,1)}, u32[]{:S(2)}, u32[]{:S(2)}) collective-permute-start(bf16[256,1024]{1,0:T(8,128)(2,1)} %get-tuple-element.125), channel_id=1, source_target_pairs={{2,0},{4,2},{6,4},{7,6},{5,7},{3,5},{1,3},{0,1},{10,8},{12,10},{14... | collective-permute-start | bytes 1572872 | tf_op jit(solution)/shard_map/ppermute | solution.py:47
  236.1 41.1 %collective-permute-start.65 = (bf16[256,1024]{1,0:T(8,128)(2,1)}, bf16[256,1024]{1,0:T(8,128)(2,1)}, u32[]{:S(2)}, u32[]{:S(2)}) collective-permute-start(bf16[256,1024]{1,0:T(8,128)(2,1)} %get-tuple-element.124), channel_id=1, source_target_pairs={{0,2},{2,4},{4,6},{6,7},{7,5},{5,3},{3,1},{1,0},{8,10},{10,12},{12... | collective-permute-start | bytes 1572872 | tf_op jit(solution)/shard_map/ppermute | solution.py:47
  249.0 35.4 %collective-permute-start.30 = (bf16[768,512]{1,0:T(8,128)(2,1)}, bf16[768,512]{1,0:T(8,128)(2,1)}, u32[]{:S(2)}, u32[]{:S(2)}) collective-permute-start(bf16[768,512]{1,0:T(8,128)(2,1)} %slice.720), channel_id=1, source_target_pairs={{0,8},{8,0},{1,9},{9,1},{2,10},{10,2},{3,11},{11,3},{4,12},{12,4},... | collective-permute-start | bytes 2359304 | tf_op jit(solution)/shard_map/ppermute | solution.py:146
  261.7 27.3 %collective-permute-start.32 = (bf16[768,1024]{1,0:T(8,128)(2,1)}, bf16[768,1024]{1,0:T(8,128)(2,1)}, u32[]{:S(2)}, u32[]{:S(2)}) collective-permute-start(bf16[768,1024]{1,0:T(8,128)(2,1)} %pad_maximum_fusion.4), channel_id=1, source_target_pairs={{0,8},{8,0},{1,9},{9,1},{2,10},{10,2},{3,11},{11,3},{4,12},{12,4},... | collective-permute-start | bytes 4718600 | tf_op jit(solution)/shard_map/ppermute | solution.py:146
  268.4 14.5 %collective-permute-start.69 = (bf16[256,1024]{1,0:T(8,128)(2,1)S(1)}, bf16[256,1024]{1,0:T(8,128)(2,1)S(1)}, u32[]{:S(2)}, u32[]{:S(2)}) collective-permute-start(bf16[256,1024]{1,0:T(8,128)(2,1)S(1)} %add_convert_fusion.9), channel_id=1, source_target_pairs={{2,0},{4,2},{6,4},{7,6},{5,7},{3,5},{1,3},{0,1},{10,8},{12,10},{14... | collective-permute-start | bytes 1572872 | tf_op jit(solution)/shard_map/ppermute | solution.py:47
  288.0 125.0 %collective-permute-start.71 = (bf16[512,512]{1,0:T(8,128)(2,1)}, bf16[512,512]{1,0:T(8,128)(2,1)}, u32[]{:S(2)}, u32[]{:S(2)}) collective-permute-start(bf16[512,512]{1,0:T(8,128)(2,1)} %pad_maximum_fusion.12), channel_id=1, source_target_pairs={{0,16},{16,0},{1,17},{17,1},{2,18},{18,2},{3,19},{19,3},{4,20},{20... | collective-permute-start | bytes 1572872 | tf_op jit(solution)/shard_map/ppermute | solution.py:414
  353.2 85.7 %collective-permute-start.33 = (bf16[1536,512]{1,0:T(8,128)(2,1)}, bf16[1536,512]{1,0:T(8,128)(2,1)}, u32[]{:S(2)}, u32[]{:S(2)}) collective-permute-start(bf16[1536,512]{1,0:T(8,128)(2,1)} %slice.718), channel_id=1, source_target_pairs={{0,8},{8,0},{1,9},{9,1},{2,10},{10,2},{3,11},{11,3},{4,12},{12,4},... | collective-permute-start | bytes 4718600 | tf_op jit(solution)/shard_map/ppermute | solution.py:146
  368.2 29.6 %collective-permute-start.53 = (bf16[320,1024]{1,0:T(8,128)(2,1)S(1)}, bf16[320,1024]{1,0:T(8,128)(2,1)S(1)}, u32[]{:S(2)}, u32[]{:S(2)}) collective-permute-start(bf16[320,1024]{1,0:T(8,128)(2,1)S(1)} %fusion.26), channel_id=1, source_target_pairs={{0,2},{2,4},{4,6},{6,7},{7,5},{5,3},{3,1},{1,0},{8,10},{10,12},{12... | collective-permute-start | bytes 1966088 | tf_op jit(solution)/shard_map/ppermute | solution.py:47
  375.7 20.1 %collective-permute-start.41 = (bf16[224,1024]{1,0:T(8,128)(2,1)S(1)}, bf16[224,1024]{1,0:T(8,128)(2,1)S(1)}, u32[]{:S(2)}, u32[]{:S(2)}) collective-permute-start(bf16[224,1024]{1,0:T(8,128)(2,1)S(1)} %fusion.29), channel_id=1, source_target_pairs={{0,2},{2,4},{4,6},{6,7},{7,5},{5,3},{3,1},{1,0},{8,10},{10,12},{12... | collective-permute-start | bytes 1376264 | tf_op jit(solution)/shard_map/ppermute | solution.py:47
  383.8 31.9 %collective-permute-start.57 = (bf16[320,1024]{1,0:T(8,128)(2,1)S(1)}, bf16[320,1024]{1,0:T(8,128)(2,1)S(1)}, u32[]{:S(2)}, u32[]{:S(2)}) collective-permute-start(bf16[320,1024]{1,0:T(8,128)(2,1)S(1)} %pad_maximum_fusion.5), channel_id=1, source_target_pairs={{2,0},{4,2},{6,4},{7,6},{5,7},{3,5},{1,3},{0,1},{10,8},{12,10},{14... | collective-permute-start | bytes 1966088 | tf_op jit(solution)/shard_map/ppermute | solution.py:47
  395.8 14.3 %collective-permute-start.46 = (bf16[224,1024]{1,0:T(8,128)(2,1)S(1)}, bf16[224,1024]{1,0:T(8,128)(2,1)S(1)}, u32[]{:S(2)}, u32[]{:S(2)}) collective-permute-start(bf16[224,1024]{1,0:T(8,128)(2,1)S(1)} %add_convert_fusion.15), channel_id=1, source_target_pairs={{2,0},{4,2},{6,4},{7,6},{5,7},{3,5},{1,3},{0,1},{10,8},{12,10},{14... | collective-permute-start | bytes 1376264 | tf_op jit(solution)/shard_map/ppermute | solution.py:47
  410.1 26.1 %collective-permute-start.54 = (bf16[320,1024]{1,0:T(8,128)(2,1)S(1)}, bf16[320,1024]{1,0:T(8,128)(2,1)S(1)}, u32[]{:S(2)}, u32[]{:S(2)}) collective-permute-start(bf16[320,1024]{1,0:T(8,128)(2,1)S(1)} %add_convert_fusion.7), channel_id=1, source_target_pairs={{0,2},{2,4},{4,6},{6,7},{7,5},{5,3},{3,1},{1,0},{8,10},{10,12},{12... | collective-permute-start | bytes 1966088 | tf_op jit(solution)/shard_map/ppermute | solution.py:47
  413.0 22.9 %collective-permute-start.43 = (bf16[224,1024]{1,0:T(8,128)(2,1)S(1)}, bf16[224,1024]{1,0:T(8,128)(2,1)S(1)}, u32[]{:S(2)}, u32[]{:S(2)}) collective-permute-start(bf16[224,1024]{1,0:T(8,128)(2,1)S(1)} %add_convert_fusion.16), channel_id=1, source_target_pairs={{0,2},{2,4},{4,6},{6,7},{7,5},{5,3},{3,1},{1,0},{8,10},{10,12},{12... | collective-permute-start | bytes 1376264 | tf_op jit(solution)/shard_map/ppermute | solution.py:47
  416.0 29.1 %collective-permute-start.58 = (bf16[320,1024]{1,0:T(8,128)(2,1)S(1)}, bf16[320,1024]{1,0:T(8,128)(2,1)S(1)}, u32[]{:S(2)}, u32[]{:S(2)}) collective-permute-start(bf16[320,1024]{1,0:T(8,128)(2,1)S(1)} %add_convert_fusion.5), channel_id=1, source_target_pairs={{2,0},{4,2},{6,4},{7,6},{5,7},{3,5},{1,3},{0,1},{10,8},{12,10},{14... | collective-permute-start | bytes 1966088 | tf_op jit(solution)/shard_map/ppermute | solution.py:47
  437.4 18.4 %collective-permute-start.55 = (bf16[320,1024]{1,0:T(8,128)(2,1)}, bf16[320,1024]{1,0:T(8,128)(2,1)}, u32[]{:S(2)}, u32[]{:S(2)}) collective-permute-start(bf16[320,1024]{1,0:T(8,128)(2,1)} %add_convert_fusion.6), channel_id=1, source_target_pairs={{0,2},{2,4},{4,6},{6,7},{7,5},{5,3},{3,1},{1,0},{8,10},{10,12},{12... | collective-permute-start | bytes 1966088 | tf_op jit(solution)/shard_map/ppermute | solution.py:47
  443.6 40.2 %collective-permute-start.34 = (bf16[768,512]{1,0:T(8,128)(2,1)}, bf16[768,512]{1,0:T(8,128)(2,1)}, u32[]{:S(2)}, u32[]{:S(2)}) collective-permute-start(bf16[768,512]{1,0:T(8,128)(2,1)} %slice.719), channel_id=1, source_target_pairs={{1,0},{2,1},{3,2},{5,4},{6,5},{7,6},{9,8},{10,9},{11,10},{13,12},{... | collective-permute-start | bytes 2359304 | tf_op jit(solution)/shard_map/ppermute | solution.py:620
  446.1 34.3 %collective-permute-start.59 = (bf16[320,1024]{1,0:T(8,128)(2,1)}, bf16[320,1024]{1,0:T(8,128)(2,1)}, u32[]{:S(2)}, u32[]{:S(2)}) collective-permute-start(bf16[320,1024]{1,0:T(8,128)(2,1)} %add_convert_fusion.4), channel_id=1, source_target_pairs={{2,0},{4,2},{6,4},{7,6},{5,7},{3,5},{1,3},{0,1},{10,8},{12,10},{14... | collective-permute-start | bytes 1966088 | tf_op jit(solution)/shard_map/ppermute | solution.py:47
  451.1 39.3 %collective-permute-start.49 = (bf16[384,512]{1,0:T(8,128)(2,1)}, bf16[384,512]{1,0:T(8,128)(2,1)}, u32[]{:S(2)}, u32[]{:S(2)}) collective-permute-start(bf16[384,512]{1,0:T(8,128)(2,1)} %pad_maximum_fusion.14), channel_id=1, source_target_pairs={{0,16},{16,0},{1,17},{17,1},{2,18},{18,2},{3,19},{19,3},{4,20},{20... | collective-permute-start | bytes 1179656 | tf_op jit(solution)/shard_map/ppermute | solution.py:414
  483.8 15.5 %collective-permute-start.60 = (bf16[320,512]{1,0:T(8,128)(2,1)}, bf16[320,512]{1,0:T(8,128)(2,1)}, u32[]{:S(2)}, u32[]{:S(2)}) collective-permute-start(bf16[320,512]{1,0:T(8,128)(2,1)} %slice.610), channel_id=1, source_target_pairs={{0,8},{8,0},{1,9},{9,1},{2,10},{10,2},{3,11},{11,3},{4,12},{12,4},... | collective-permute-start | bytes 983048 | tf_op jit(solution)/shard_map/ppermute | solution.py:146
  500.4 15.3 %collective-permute-start.61 = (bf16[640,512]{1,0:T(8,128)(2,1)S(1)}, bf16[640,512]{1,0:T(8,128)(2,1)S(1)}, u32[]{:S(2)}, u32[]{:S(2)}) collective-permute-start(bf16[640,512]{1,0:T(8,128)(2,1)S(1)} %pad_maximum_fusion.6), channel_id=1, source_target_pairs={{0,16},{16,0},{1,17},{17,1},{2,18},{18,2},{3,19},{19,3},{4,20},{20... | collective-permute-start | bytes 1966088 | tf_op jit(solution)/shard_map/ppermute | solution.py:414
  (118 other events, 1258.3 us)
